TPU v7x, 512 devices: a whole 4x4x16 slice. The times are simulated.
512 devices in a mesh: head: 16 (over z_hi, y, core), seq: 32 (over z_lo, x).
Axes of the slice: x: 4, y: 4, z: 16 (z_hi: 2, z_lo: 8; z = z_hi * 8 + z_lo), core: 2. Of those that a mesh axis runs over, the one named last changes fastest.
Arguments:
- query_rows: bfloat16 [4096, 3072], P(('seq', 'head')), may hold values from -6 to 6
- key_rows: bfloat16 [4096, 3072], P(('seq', 'head')), may hold values from -6 to 6
- value_rows: bfloat16 [4096, 3072], P(('seq', 'head')), may hold values from -6 to 6
- gate_rows: bfloat16 [4096, 3072], P(('seq', 'head')), may hold values from -1 to 1
- step_rates: float32 [4096, 48], P('seq', 'head'), may hold values from 5e-05 to 0.0005
- first_weight: float32 [48, 64, 256], P('head'), may hold values from -0.75 to 0.75
- first_bias: float32 [48, 256], P('head'), may hold values from -3 to 3
- second_weight: float32 [48, 256, 64], P('head'), may hold values from -0.375 to 0.375
- second_bias: float32 [48, 64], P('head'), may hold values from -3 to 3
- norm_gain: float32 [48, 64], P('head'), may hold values from 0.5 to 1.5
- norm_shift: float32 [48, 64], P('head'), may hold values from -3 to 3
Outputs:
- layer_output: bfloat16 [4096, 3072], P(('seq', 'head'))
All inputs are finite; a program needn't handle non-finite values.
Results may differ from a plain program's by a relative error of at most 0.0049.
Values may be sent and summed in bfloat16 or wider, within the bound.
A program may use at most 64 MiB of HBM per device.

v0:
```python
import jax
import jax.numpy as jnp
from jax import lax
from jax.sharding import PartitionSpec as P

D_HEAD = 64
INNER = 256
MINI = 64


highest = lax.Precision.HIGHEST
eps_norm = 1e-06
root_factor = 0.7978845608028654
cube_factor = 0.044715


def shifted(block, axis, distance):
    devices = range(lax.axis_size(axis))
    route = [(i - distance, i) for i in devices if i - distance in devices]
    return lax.ppermute(block, axis, route)


def gelu_tanh(values):
    tanh_term = jnp.tanh(root_factor * (values + cube_factor * values * values * values))
    return 0.5 * values * (1.0 + tanh_term)


def gelu_slope(values):
    tanh_term = jnp.tanh(root_factor * (values + cube_factor * values * values * values))
    return 0.5 * (1.0 + tanh_term) + 0.5 * values * (1.0 - tanh_term * tanh_term) * root_factor * (
        1.0 + 3.0 * cube_factor * values * values
    )


def layer_norm(values, gain_row, shift_row):
    centred = values - jnp.mean(values, axis=-1, keepdims=True)
    spread = jnp.sqrt(jnp.mean(centred * centred, axis=-1, keepdims=True) + eps_norm)
    normed = centred / spread
    return (normed, spread, gain_row * normed + shift_row)


def unpack(fast_state):
    weight_one = fast_state[:D_HEAD]
    second_turned = fast_state[D_HEAD : 2 * D_HEAD]
    bias_one = fast_state[2 * D_HEAD]
    bias_two = fast_state[2 * D_HEAD + 1, :D_HEAD]
    return (weight_one, bias_one, second_turned, bias_two)


def gradients(fast_state, key_block, value_block, gain_row, shift_row):
    weight_one, bias_one, second_turned, bias_two = unpack(fast_state)
    pre_one = jnp.dot(key_block, weight_one, precision=highest) + bias_one
    act_one = gelu_tanh(pre_one)
    pre_two = jnp.einsum("ti,di->td", act_one, second_turned, precision=highest) + bias_two
    normed, spread, fitted = layer_norm(pre_two, gain_row, shift_row)
    scaled = gain_row * (fitted - (value_block - key_block))
    grad_two = (
        scaled
        - jnp.mean(scaled, axis=-1, keepdims=True)
        - normed * jnp.mean(scaled * normed, axis=-1, keepdims=True)
    ) / spread
    grad_one = jnp.dot(grad_two, second_turned, precision=highest) * gelu_slope(pre_one)
    return (act_one, grad_one, grad_two)


def renew(fast_state, key_block, act_one, grad_one, grad_two, rate_row):
    weight_one, bias_one, second_turned, bias_two = unpack(fast_state)
    weighted_one = rate_row[:, None] * grad_one
    weighted_two = rate_row[:, None] * grad_two
    new_first = weight_one - jnp.einsum("td,ti->di", key_block, weighted_one, precision=highest)
    new_second = second_turned - jnp.einsum("td,ti->di", weighted_two, act_one, precision=highest)
    new_bias_one = bias_one - jnp.sum(weighted_one, axis=0)
    new_bias_two = bias_two - jnp.sum(weighted_two, axis=0)
    filler = jnp.zeros((fast_state.shape[1] - D_HEAD,), jnp.float32)
    return jnp.concatenate(
        [
            new_first,
            new_second,
            new_bias_one[None, :],
            jnp.concatenate([new_bias_two, filler])[None, :],
        ],
        axis=0,
    )


def dual_output(
    fast_state, query_block, key_block, act_one, grad_one, grad_two, rate_row, gain_row, shift_row
):
    weight_one, bias_one, second_turned, bias_two = unpack(fast_state)
    lower_mask = jnp.arange(MINI)[:, None] >= jnp.arange(MINI)[None, :]
    step_matrix = jnp.where(lower_mask, rate_row[None, :], 0.0)
    attend_one = (
        jnp.einsum("sd,td->st", query_block, key_block, precision=highest) + 1.0
    ) * step_matrix
    dual_one = (
        jnp.dot(query_block, weight_one, precision=highest)
        + bias_one
        - jnp.dot(attend_one, grad_one, precision=highest)
    )
    dual_act = gelu_tanh(dual_one)
    attend_two = (jnp.einsum("si,ti->st", dual_act, act_one, precision=highest) + 1.0) * step_matrix
    dual_two = (
        jnp.einsum("si,di->sd", dual_act, second_turned, precision=highest)
        + bias_two
        - jnp.dot(attend_two, grad_two, precision=highest)
    )
    return layer_norm(dual_two, gain_row, shift_row)[2]


def orient(array_in, reverse):
    if reverse:
        return jnp.flip(array_in, 0)
    return array_in


def to_blocks(array_in):
    block_count = array_in.shape[0] // MINI
    return array_in.reshape((block_count, MINI) + array_in.shape[1:])


def segment(fast_state, query_head, key_head, value_head, rate_head, gain_row, shift_row):

    def advance(carried, block_data):
        query_block = block_data[0].astype(jnp.float32)
        key_block = block_data[1].astype(jnp.float32)
        value_block = block_data[2].astype(jnp.float32)
        rate_row = block_data[3]
        act_one, grad_one, grad_two = gradients(
            carried, key_block, value_block, gain_row, shift_row
        )
        updated = renew(carried, key_block, act_one, grad_one, grad_two, rate_row)
        emitted = dual_output(
            carried,
            query_block,
            key_block,
            act_one,
            grad_one,
            grad_two,
            rate_row,
            gain_row,
            shift_row,
        )
        return (updated, emitted)

    return lax.scan(
        advance,
        fast_state,
        (to_blocks(query_head), to_blocks(key_head), to_blocks(value_head), to_blocks(rate_head)),
    )


def local(
    query_rows,
    key_rows,
    value_rows,
    gate_rows,
    step_rates,
    first_weight,
    first_bias,
    second_weight,
    second_bias,
    norm_gain,
    norm_shift,
):
    query_local, key_local, value_local, gate_local = (
        lax.all_to_all(query_rows, "head", split_axis=1, concat_axis=0, tiled=True),
        lax.all_to_all(key_rows, "head", split_axis=1, concat_axis=0, tiled=True),
        lax.all_to_all(value_rows, "head", split_axis=1, concat_axis=0, tiled=True),
        lax.all_to_all(gate_rows, "head", split_axis=1, concat_axis=0, tiled=True),
    )
    token_count = query_local.shape[0]
    heads_local = step_rates.shape[1]
    query_heads = query_local.reshape(token_count, heads_local, D_HEAD)
    key_heads = key_local.reshape(token_count, heads_local, D_HEAD)
    value_heads = value_local.reshape(token_count, heads_local, D_HEAD)
    filler = jnp.zeros((heads_local, 1, INNER - D_HEAD), jnp.float32)
    initial = jnp.concatenate(
        [
            first_weight,
            jnp.swapaxes(second_weight, 1, 2),
            first_bias[:, None, :],
            jnp.concatenate([second_bias[:, None, :], filler], axis=2),
        ],
        axis=1,
    )
    state_rows = 2 * D_HEAD + 2
    position = lax.axis_index("seq")
    chain_size = lax.axis_size("seq")
    store_shape = (token_count, heads_local, D_HEAD)
    blank_store = jnp.zeros(store_shape, jnp.float32)

    def direction_turn(section_turn, received, stored, first_device, chain_place, reverse):
        head_now = section_turn - chain_place
        active = jnp.logical_and(head_now >= 0, head_now < heads_local)
        chosen = jnp.clip(head_now, 0, heads_local - 1)
        starting = jnp.where(
            first_device, lax.dynamic_index_in_dim(initial, chosen, 0, keepdims=False), received
        )

        def work(operands):
            start_state, kept = operands
            query_head = orient(
                lax.dynamic_index_in_dim(query_heads, chosen, 1, keepdims=False), reverse
            )
            key_head = orient(
                lax.dynamic_index_in_dim(key_heads, chosen, 1, keepdims=False), reverse
            )
            value_head = orient(
                lax.dynamic_index_in_dim(value_heads, chosen, 1, keepdims=False), reverse
            )
            rate_head = orient(
                lax.dynamic_index_in_dim(step_rates, chosen, 1, keepdims=False), reverse
            )
            gain_row = lax.dynamic_index_in_dim(norm_gain, chosen, 0, keepdims=False)
            shift_row = lax.dynamic_index_in_dim(norm_shift, chosen, 0, keepdims=False)
            finished, emitted = segment(
                start_state, query_head, key_head, value_head, rate_head, gain_row, shift_row
            )
            rows_out = orient(emitted.reshape(token_count, D_HEAD), reverse)
            kept = lax.dynamic_update_slice(kept, rows_out[:, None, :], (0, chosen, 0))
            return (finished, kept)

        def skip(operands):
            return (jnp.zeros_like(operands[0]), operands[1])

        return lax.cond(active, work, skip, (starting, stored))

    def turn_body(section_turn, loop_state):
        received_ahead, received_back, store_ahead, store_back = loop_state
        sent_ahead, store_ahead = direction_turn(
            section_turn, received_ahead, store_ahead, position == 0, position, False
        )
        sent_back, store_back = direction_turn(
            section_turn,
            received_back,
            store_back,
            position == chain_size - 1,
            chain_size - 1 - position,
            True,
        )
        received_ahead = shifted(sent_ahead, "seq", 1)
        received_back = shifted(sent_back, "seq", -1)
        return (received_ahead, received_back, store_ahead, store_back)

    empty_state = jnp.zeros((state_rows, INNER), jnp.float32)
    loop_state = lax.fori_loop(
        0,
        chain_size + heads_local - 1,
        turn_body,
        (empty_state, empty_state, blank_store, blank_store),
    )
    store_ahead = loop_state[2]
    store_back = loop_state[3]
    combined = store_ahead + store_back
    summed = combined.reshape(token_count, heads_local * D_HEAD).astype(jnp.bfloat16)
    summed = lax.optimization_barrier(summed)
    gated = (gate_local.astype(jnp.float32) * summed.astype(jnp.float32)).astype(jnp.bfloat16)
    return lax.all_to_all(gated, "head", split_axis=0, concat_axis=1, tiled=True)


def solution(mesh):
    in_specs = (
        P(("seq", "head"), None),
        P(("seq", "head"), None),
        P(("seq", "head"), None),
        P(("seq", "head"), None),
        P("seq", "head"),
        P("head", None, None),
        P("head", None),
        P("head", None, None),
        P("head", None),
        P("head", None),
        P("head", None),
    )
    out_specs = P(("seq", "head"), None)
    return jax.shard_map(local, mesh=mesh, in_specs=in_specs, out_specs=out_specs, check_vma=False)
```

profile of v0, /device:TPU:231, one launch (start us, length us, event | category | flops | bytes accessed | tf_op | source)
XLA Modules:
  0.0 1493.8 jit_solution(7031491233722609634)
XLA Ops:
  1.6 11.0 all-to-all-start.1
  13.4 13.7 all-to-all-done.1
  31.7 13.8 all-to-all-done.2
  50.4 13.4 all-to-all-done.3
  68.6 1351.1 %while.66 = (s32[]{:T(128)}, f32[130,256]{1,0:T(8,128)S(1)}, f32[130,256]{1,0:T(8,128)S(1)}, f32[128,3,64]{2,1,0:T(4,128)S(1)}, f32[128,3,64]{2,1,0:T(4,128)S(1)...) while((s32[]{:T(128)}, f32[130,256]{1,0:T(8,128)S(1)}, ...), condition=%wide.region_25.26_spmd, body=%wide.region_0.25_spmd.sunk | while | flops 236359936 | bytes 7138877 | solution.py:246
  68.6 27.4 %conditional.5 = (f32[130,256]{1,0:T(8,128)}, f32[128,3,64]{2,1,0:T(4,128)S(1)}) conditional(s32[]{:T(128)} %convert_element_type.85, f32[128,3,64]{2,1,0:T(4,128)S(1)} %get-tuple-element.1107, (pred[]{:T(512)}, s32[]{:T(128)}, f32[3,130,256]{2,1,0:T(8,128)S(1)}, f32[130,256]{1,0:T(8,128)S(1)}, bf16[128,3,64]{2,0,1:T(8,128)(2,1)S(1)}, ...), branch_computations={%region_13.13_spmd, %region_14.24_spmd} | conditional | flops 118179968 | bytes 3119138 | solution.py:226
  69.9 24.6 %while.65 = (s32[]{:T(128)}, f32[130,256]{1,0:T(8,128)}, f32[2,64,64]{2,1,0:T(8,128)S(1)}, bf16[2,64,64]{1,2,0:T(8,128)(2,1)S(1)}, f32[2,64]{1,0:T(2,128)S(1)}, ...) while((s32[]{:T(128)}, f32[130,256]{1,0:T(8,128)}, ...), condition=%wide.region_24.23_spmd, body=%wide.region_15.22_spmd.sunk | while | flops 118146688 | bytes 2256769 | solution.py:145
  105.1 27.4 %conditional.5 = (f32[130,256]{1,0:T(8,128)}, f32[128,3,64]{2,1,0:T(4,128)S(1)}) conditional(s32[]{:T(128)} %convert_element_type.85, f32[128,3,64]{2,1,0:T(4,128)S(1)} %get-tuple-element.1107, (pred[]{:T(512)}, s32[]{:T(128)}, f32[3,130,256]{2,1,0:T(8,128)S(1)}, f32[130,256]{1,0:T(8,128)S(1)}, bf16[128,3,64]{2,0,1:T(8,128)(2,1)S(1)}, ...), branch_computations={%region_13.13_spmd, %region_14.24_spmd} | conditional | flops 118179968 | bytes 3119138 | solution.py:226
  106.4 24.6 %while.65 = (s32[]{:T(128)}, f32[130,256]{1,0:T(8,128)}, f32[2,64,64]{2,1,0:T(8,128)S(1)}, bf16[2,64,64]{1,2,0:T(8,128)(2,1)S(1)}, f32[2,64]{1,0:T(2,128)S(1)}, ...) while((s32[]{:T(128)}, f32[130,256]{1,0:T(8,128)}, ...), condition=%wide.region_24.23_spmd, body=%wide.region_15.22_spmd.sunk | while | flops 118146688 | bytes 2256769 | solution.py:145
  140.6 27.4 %conditional.5 = (f32[130,256]{1,0:T(8,128)}, f32[128,3,64]{2,1,0:T(4,128)S(1)}) conditional(s32[]{:T(128)} %convert_element_type.85, f32[128,3,64]{2,1,0:T(4,128)S(1)} %get-tuple-element.1107, (pred[]{:T(512)}, s32[]{:T(128)}, f32[3,130,256]{2,1,0:T(8,128)S(1)}, f32[130,256]{1,0:T(8,128)S(1)}, bf16[128,3,64]{2,0,1:T(8,128)(2,1)S(1)}, ...), branch_computations={%region_13.13_spmd, %region_14.24_spmd} | conditional | flops 118179968 | bytes 3119138 | solution.py:226
  141.9 24.6 %while.65 = (s32[]{:T(128)}, f32[130,256]{1,0:T(8,128)}, f32[2,64,64]{2,1,0:T(8,128)S(1)}, bf16[2,64,64]{1,2,0:T(8,128)(2,1)S(1)}, f32[2,64]{1,0:T(2,128)S(1)}, ...) while((s32[]{:T(128)}, f32[130,256]{1,0:T(8,128)}, ...), condition=%wide.region_24.23_spmd, body=%wide.region_15.22_spmd.sunk | while | flops 118146688 | bytes 2256769 | solution.py:145
  177.3 29.0 %collective-permute-start.1 = (f32[130,256]{1,0:T(8,128)}, f32[130,256]{1,0:T(8,128)S(1)}, u32[]{:S(2)}, u32[]{:S(2)}) collective-permute-start(f32[130,256]{1,0:T(8,128)} %get-tuple-element.963), channel_id=1, source_target_pairs={{1,0},{2,1},{3,2},{4,3},{5,4},{6,5},{7,6},{8,7},{9,8},{10,9},{11,1... | collective-permute-start | bytes 399368 | tf_op jit(solution)/shard_map/while/body/eval_jaxpr/ppermute | solution.py:20
  218.1 29.4 %collective-permute-done = f32[130,256]{1,0:T(8,128)S(1)} collective-permute-done((f32[130,256]{1,0:T(8,128)}, f32[130,256]{1,0:T(8,128)S(1)}, u32[]{:S(2)}, u32[]{:S(2)}) %collective-permute-start) | collective-permute-done | bytes 133152 | tf_op jit(solution)/shard_map/while/body/eval_jaxpr/ppermute | solution.py:20
  258.9 30.5 %collective-permute-start.1 = (f32[130,256]{1,0:T(8,128)}, f32[130,256]{1,0:T(8,128)S(1)}, u32[]{:S(2)}, u32[]{:S(2)}) collective-permute-start(f32[130,256]{1,0:T(8,128)} %get-tuple-element.963), channel_id=1, source_target_pairs={{1,0},{2,1},{3,2},{4,3},{5,4},{6,5},{7,6},{8,7},{9,8},{10,9},{11,1... | collective-permute-start | bytes 399368 | tf_op jit(solution)/shard_map/while/body/eval_jaxpr/ppermute | solution.py:20
  303.1 29.4 %collective-permute-done = f32[130,256]{1,0:T(8,128)S(1)} collective-permute-done((f32[130,256]{1,0:T(8,128)}, f32[130,256]{1,0:T(8,128)S(1)}, u32[]{:S(2)}, u32[]{:S(2)}) %collective-permute-start) | collective-permute-done | bytes 133152 | tf_op jit(solution)/shard_map/while/body/eval_jaxpr/ppermute | solution.py:20
  333.2 5.5 collective-permute-start.1
  346.3 24.5 %collective-permute-start.1 = (f32[130,256]{1,0:T(8,128)}, f32[130,256]{1,0:T(8,128)S(1)}, u32[]{:S(2)}, u32[]{:S(2)}) collective-permute-start(f32[130,256]{1,0:T(8,128)} %get-tuple-element.963), channel_id=1, source_target_pairs={{1,0},{2,1},{3,2},{4,3},{5,4},{6,5},{7,6},{8,7},{9,8},{10,9},{11,1... | collective-permute-start | bytes 399368 | tf_op jit(solution)/shard_map/while/body/eval_jaxpr/ppermute | solution.py:20
  378.1 5.5 collective-permute-start.1
  385.9 25.8 %collective-permute-done = f32[130,256]{1,0:T(8,128)S(1)} collective-permute-done((f32[130,256]{1,0:T(8,128)}, f32[130,256]{1,0:T(8,128)S(1)}, u32[]{:S(2)}, u32[]{:S(2)}) %collective-permute-start) | collective-permute-done | bytes 133152 | tf_op jit(solution)/shard_map/while/body/eval_jaxpr/ppermute | solution.py:20
  412.4 5.5 collective-permute-start.1
  425.2 24.8 %collective-permute-start.1 = (f32[130,256]{1,0:T(8,128)}, f32[130,256]{1,0:T(8,128)S(1)}, u32[]{:S(2)}, u32[]{:S(2)}) collective-permute-start(f32[130,256]{1,0:T(8,128)} %get-tuple-element.963), channel_id=1, source_target_pairs={{1,0},{2,1},{3,2},{4,3},{5,4},{6,5},{7,6},{8,7},{9,8},{10,9},{11,1... | collective-permute-start | bytes 399368 | tf_op jit(solution)/shard_map/while/body/eval_jaxpr/ppermute | solution.py:20
  457.4 5.5 collective-permute-start.1
  466.2 26.9 %collective-permute-done = f32[130,256]{1,0:T(8,128)S(1)} collective-permute-done((f32[130,256]{1,0:T(8,128)}, f32[130,256]{1,0:T(8,128)S(1)}, u32[]{:S(2)}, u32[]{:S(2)}) %collective-permute-start) | collective-permute-done | bytes 133152 | tf_op jit(solution)/shard_map/while/body/eval_jaxpr/ppermute | solution.py:20
  493.8 5.5 collective-permute-start.1
  501.6 6.5 collective-permute-done
  508.7 22.7 %collective-permute-start.1 = (f32[130,256]{1,0:T(8,128)}, f32[130,256]{1,0:T(8,128)S(1)}, u32[]{:S(2)}, u32[]{:S(2)}) collective-permute-start(f32[130,256]{1,0:T(8,128)} %get-tuple-element.963), channel_id=1, source_target_pairs={{1,0},{2,1},{3,2},{4,3},{5,4},{6,5},{7,6},{8,7},{9,8},{10,9},{11,1... | collective-permute-start | bytes 399368 | tf_op jit(solution)/shard_map/while/body/eval_jaxpr/ppermute | solution.py:20
  538.8 8.4 collective-permute-start.1
  549.5 22.9 %collective-permute-done = f32[130,256]{1,0:T(8,128)S(1)} collective-permute-done((f32[130,256]{1,0:T(8,128)}, f32[130,256]{1,0:T(8,128)S(1)}, u32[]{:S(2)}, u32[]{:S(2)}) %collective-permute-start) | collective-permute-done | bytes 133152 | tf_op jit(solution)/shard_map/while/body/eval_jaxpr/ppermute | solution.py:20
  573.0 5.5 collective-permute-start.1
  580.8 6.1 collective-permute-done
  587.6 23.1 %collective-permute-start.1 = (f32[130,256]{1,0:T(8,128)}, f32[130,256]{1,0:T(8,128)S(1)}, u32[]{:S(2)}, u32[]{:S(2)}) collective-permute-start(f32[130,256]{1,0:T(8,128)} %get-tuple-element.963), channel_id=1, source_target_pairs={{1,0},{2,1},{3,2},{4,3},{5,4},{6,5},{7,6},{8,7},{9,8},{10,9},{11,1... | collective-permute-start | bytes 399368 | tf_op jit(solution)/shard_map/while/body/eval_jaxpr/ppermute | solution.py:20
  618.0 6.0 collective-permute-start.1
  626.4 27.4 %collective-permute-done = f32[130,256]{1,0:T(8,128)S(1)} collective-permute-done((f32[130,256]{1,0:T(8,128)}, f32[130,256]{1,0:T(8,128)S(1)}, u32[]{:S(2)}, u32[]{:S(2)}) %collective-permute-start) | collective-permute-done | bytes 133152 | tf_op jit(solution)/shard_map/while/body/eval_jaxpr/ppermute | solution.py:20
  654.4 5.5 collective-permute-start.1
  662.2 6.4 collective-permute-done
  669.3 22.8 %collective-permute-start.1 = (f32[130,256]{1,0:T(8,128)}, f32[130,256]{1,0:T(8,128)S(1)}, u32[]{:S(2)}, u32[]{:S(2)}) collective-permute-start(f32[130,256]{1,0:T(8,128)} %get-tuple-element.963), channel_id=1, source_target_pairs={{1,0},{2,1},{3,2},{4,3},{5,4},{6,5},{7,6},{8,7},{9,8},{10,9},{11,1... | collective-permute-start | bytes 399368 | tf_op jit(solution)/shard_map/while/body/eval_jaxpr/ppermute | solution.py:20
  699.4 6.0 collective-permute-start.1
  707.7 25.3 %collective-permute-done = f32[130,256]{1,0:T(8,128)S(1)} collective-permute-done((f32[130,256]{1,0:T(8,128)}, f32[130,256]{1,0:T(8,128)S(1)}, u32[]{:S(2)}, u32[]{:S(2)}) %collective-permute-start) | collective-permute-done | bytes 133152 | tf_op jit(solution)/shard_map/while/body/eval_jaxpr/ppermute | solution.py:20
  733.7 25.6 %collective-permute-start.1 = (f32[130,256]{1,0:T(8,128)}, f32[130,256]{1,0:T(8,128)S(1)}, u32[]{:S(2)}, u32[]{:S(2)}) collective-permute-start(f32[130,256]{1,0:T(8,128)} %get-tuple-element.963), channel_id=1, source_target_pairs={{1,0},{2,1},{3,2},{4,3},{5,4},{6,5},{7,6},{8,7},{9,8},{10,9},{11,1... | collective-permute-start | bytes 399368 | tf_op jit(solution)/shard_map/while/body/eval_jaxpr/ppermute | solution.py:20
  761.6 30.8 %collective-permute-done = f32[130,256]{1,0:T(8,128)S(1)} collective-permute-done((f32[130,256]{1,0:T(8,128)}, f32[130,256]{1,0:T(8,128)S(1)}, u32[]{:S(2)}, u32[]{:S(2)}) %collective-permute-start) | collective-permute-done | bytes 133152 | tf_op jit(solution)/shard_map/while/body/eval_jaxpr/ppermute | solution.py:20
  793.0 59.9 %collective-permute-start.1 = (f32[130,256]{1,0:T(8,128)}, f32[130,256]{1,0:T(8,128)S(1)}, u32[]{:S(2)}, u32[]{:S(2)}) collective-permute-start(f32[130,256]{1,0:T(8,128)} %get-tuple-element.963), channel_id=1, source_target_pairs={{1,0},{2,1},{3,2},{4,3},{5,4},{6,5},{7,6},{8,7},{9,8},{10,9},{11,1... | collective-permute-start | bytes 399368 | tf_op jit(solution)/shard_map/while/body/eval_jaxpr/ppermute | solution.py:20
  855.2 30.8 %collective-permute-done = f32[130,256]{1,0:T(8,128)S(1)} collective-permute-done((f32[130,256]{1,0:T(8,128)}, f32[130,256]{1,0:T(8,128)S(1)}, u32[]{:S(2)}, u32[]{:S(2)}) %collective-permute-start) | collective-permute-done | bytes 133152 | tf_op jit(solution)/shard_map/while/body/eval_jaxpr/ppermute | solution.py:20
  886.7 31.6 %collective-permute-start.1 = (f32[130,256]{1,0:T(8,128)}, f32[130,256]{1,0:T(8,128)S(1)}, u32[]{:S(2)}, u32[]{:S(2)}) collective-permute-start(f32[130,256]{1,0:T(8,128)} %get-tuple-element.963), channel_id=1, source_target_pairs={{1,0},{2,1},{3,2},{4,3},{5,4},{6,5},{7,6},{8,7},{9,8},{10,9},{11,1... | collective-permute-start | bytes 399368 | tf_op jit(solution)/shard_map/while/body/eval_jaxpr/ppermute | solution.py:20
  920.6 55.8 %collective-permute-done = f32[130,256]{1,0:T(8,128)S(1)} collective-permute-done((f32[130,256]{1,0:T(8,128)}, f32[130,256]{1,0:T(8,128)S(1)}, u32[]{:S(2)}, u32[]{:S(2)}) %collective-permute-start) | collective-permute-done | bytes 133152 | tf_op jit(solution)/shard_map/while/body/eval_jaxpr/ppermute | solution.py:20
  977.1 33.1 %collective-permute-start.1 = (f32[130,256]{1,0:T(8,128)}, f32[130,256]{1,0:T(8,128)S(1)}, u32[]{:S(2)}, u32[]{:S(2)}) collective-permute-start(f32[130,256]{1,0:T(8,128)} %get-tuple-element.963), channel_id=1, source_target_pairs={{1,0},{2,1},{3,2},{4,3},{5,4},{6,5},{7,6},{8,7},{9,8},{10,9},{11,1... | collective-permute-start | bytes 399368 | tf_op jit(solution)/shard_map/while/body/eval_jaxpr/ppermute | solution.py:20
  1012.5 30.8 %collective-permute-done = f32[130,256]{1,0:T(8,128)S(1)} collective-permute-done((f32[130,256]{1,0:T(8,128)}, f32[130,256]{1,0:T(8,128)S(1)}, u32[]{:S(2)}, u32[]{:S(2)}) %collective-permute-start) | collective-permute-done | bytes 133152 | tf_op jit(solution)/shard_map/while/body/eval_jaxpr/ppermute | solution.py:20
  1044.0 31.9 %collective-permute-start.1 = (f32[130,256]{1,0:T(8,128)}, f32[130,256]{1,0:T(8,128)S(1)}, u32[]{:S(2)}, u32[]{:S(2)}) collective-permute-start(f32[130,256]{1,0:T(8,128)} %get-tuple-element.963), channel_id=1, source_target_pairs={{1,0},{2,1},{3,2},{4,3},{5,4},{6,5},{7,6},{8,7},{9,8},{10,9},{11,1... | collective-permute-start | bytes 399368 | tf_op jit(solution)/shard_map/while/body/eval_jaxpr/ppermute | solution.py:20
  1078.1 30.8 %collective-permute-done = f32[130,256]{1,0:T(8,128)S(1)} collective-permute-done((f32[130,256]{1,0:T(8,128)}, f32[130,256]{1,0:T(8,128)S(1)}, u32[]{:S(2)}, u32[]{:S(2)}) %collective-permute-start) | collective-permute-done | bytes 133152 | tf_op jit(solution)/shard_map/while/body/eval_jaxpr/ppermute | solution.py:20
  1109.6 31.9 %collective-permute-start.1 = (f32[130,256]{1,0:T(8,128)}, f32[130,256]{1,0:T(8,128)S(1)}, u32[]{:S(2)}, u32[]{:S(2)}) collective-permute-start(f32[130,256]{1,0:T(8,128)} %get-tuple-element.963), channel_id=1, source_target_pairs={{1,0},{2,1},{3,2},{4,3},{5,4},{6,5},{7,6},{8,7},{9,8},{10,9},{11,1... | collective-permute-start | bytes 399368 | tf_op jit(solution)/shard_map/while/body/eval_jaxpr/ppermute | solution.py:20
  1143.8 31.1 %collective-permute-done = f32[130,256]{1,0:T(8,128)S(1)} collective-permute-done((f32[130,256]{1,0:T(8,128)}, f32[130,256]{1,0:T(8,128)S(1)}, u32[]{:S(2)}, u32[]{:S(2)}) %collective-permute-start) | collective-permute-done | bytes 133152 | tf_op jit(solution)/shard_map/while/body/eval_jaxpr/ppermute | solution.py:20
  1175.5 30.1 %collective-permute-start.1 = (f32[130,256]{1,0:T(8,128)}, f32[130,256]{1,0:T(8,128)S(1)}, u32[]{:S(2)}, u32[]{:S(2)}) collective-permute-start(f32[130,256]{1,0:T(8,128)} %get-tuple-element.963), channel_id=1, source_target_pairs={{1,0},{2,1},{3,2},{4,3},{5,4},{6,5},{7,6},{8,7},{9,8},{10,9},{11,1... | collective-permute-start | bytes 399368 | tf_op jit(solution)/shard_map/while/body/eval_jaxpr/ppermute | solution.py:20
  1208.0 30.8 %collective-permute-done = f32[130,256]{1,0:T(8,128)S(1)} collective-permute-done((f32[130,256]{1,0:T(8,128)}, f32[130,256]{1,0:T(8,128)S(1)}, u32[]{:S(2)}, u32[]{:S(2)}) %collective-permute-start) | collective-permute-done | bytes 133152 | tf_op jit(solution)/shard_map/while/body/eval_jaxpr/ppermute | solution.py:20
  1239.4 31.9 %collective-permute-start.1 = (f32[130,256]{1,0:T(8,128)}, f32[130,256]{1,0:T(8,128)S(1)}, u32[]{:S(2)}, u32[]{:S(2)}) collective-permute-start(f32[130,256]{1,0:T(8,128)} %get-tuple-element.963), channel_id=1, source_target_pairs={{1,0},{2,1},{3,2},{4,3},{5,4},{6,5},{7,6},{8,7},{9,8},{10,9},{11,1... | collective-permute-start | bytes 399368 | tf_op jit(solution)/shard_map/while/body/eval_jaxpr/ppermute | solution.py:20
  1273.6 30.8 %collective-permute-done = f32[130,256]{1,0:T(8,128)S(1)} collective-permute-done((f32[130,256]{1,0:T(8,128)}, f32[130,256]{1,0:T(8,128)S(1)}, u32[]{:S(2)}, u32[]{:S(2)}) %collective-permute-start) | collective-permute-done | bytes 133152 | tf_op jit(solution)/shard_map/while/body/eval_jaxpr/ppermute | solution.py:20
  1305.1 6.1 collective-permute-start.1
  1311.2 27.1 %conditional.4 = (f32[130,256]{1,0:T(8,128)}, f32[128,3,64]{2,1,0:T(4,128)S(1)}) conditional(s32[]{:T(128)} %convert_element_type.84, f32[128,3,64]{2,1,0:T(4,128)S(1)} %get-tuple-element.1106, (pred[]{:T(512)}, s32[]{:T(128)}, f32[3,130,256]{2,1,0:T(8,128)S(1)}, f32[130,256]{1,0:T(8,128)S(1)}, bf16[128,3,64]{2,0,1:T(8,128)(2,1)S(1)}, ...), branch_computations={%region_1.1_spmd, %region_2.12_spmd} | conditional | flops 118179968 | bytes 2954274 | solution.py:226
  1312.2 24.5 %while.64 = (s32[]{:T(128)}, f32[130,256]{1,0:T(8,128)}, f32[2,64,64]{2,1,0:T(8,128)S(1)}, bf16[2,64,64]{1,2,0:T(8,128)(2,1)S(1)}, f32[2,64]{1,0:T(2,128)S(1)}, ...) while((s32[]{:T(128)}, f32[130,256]{1,0:T(8,128)}, ...), condition=%wide.region_12.11_spmd, body=%wide.region_3.10_spmd.sunk | while | flops 118146688 | bytes 2256769 | solution.py:145
  1339.6 4.7 collective-permute-done
  1349.5 27.1 %conditional.4 = (f32[130,256]{1,0:T(8,128)}, f32[128,3,64]{2,1,0:T(4,128)S(1)}) conditional(s32[]{:T(128)} %convert_element_type.84, f32[128,3,64]{2,1,0:T(4,128)S(1)} %get-tuple-element.1106, (pred[]{:T(512)}, s32[]{:T(128)}, f32[3,130,256]{2,1,0:T(8,128)S(1)}, f32[130,256]{1,0:T(8,128)S(1)}, bf16[128,3,64]{2,0,1:T(8,128)(2,1)S(1)}, ...), branch_computations={%region_1.1_spmd, %region_2.12_spmd} | conditional | flops 118179968 | bytes 2954274 | solution.py:226
  1350.5 24.5 %while.64 = (s32[]{:T(128)}, f32[130,256]{1,0:T(8,128)}, f32[2,64,64]{2,1,0:T(8,128)S(1)}, bf16[2,64,64]{1,2,0:T(8,128)(2,1)S(1)}, f32[2,64]{1,0:T(2,128)S(1)}, ...) while((s32[]{:T(128)}, f32[130,256]{1,0:T(8,128)}, ...), condition=%wide.region_12.11_spmd, body=%wide.region_3.10_spmd.sunk | while | flops 118146688 | bytes 2256769 | solution.py:145
  1377.9 4.7 collective-permute-done
  1386.6 27.1 %conditional.4 = (f32[130,256]{1,0:T(8,128)}, f32[128,3,64]{2,1,0:T(4,128)S(1)}) conditional(s32[]{:T(128)} %convert_element_type.84, f32[128,3,64]{2,1,0:T(4,128)S(1)} %get-tuple-element.1106, (pred[]{:T(512)}, s32[]{:T(128)}, f32[3,130,256]{2,1,0:T(8,128)S(1)}, f32[130,256]{1,0:T(8,128)S(1)}, bf16[128,3,64]{2,0,1:T(8,128)(2,1)S(1)}, ...), branch_computations={%region_1.1_spmd, %region_2.12_spmd} | conditional | flops 118179968 | bytes 2954274 | solution.py:226
  1387.6 24.5 %while.64 = (s32[]{:T(128)}, f32[130,256]{1,0:T(8,128)}, f32[2,64,64]{2,1,0:T(8,128)S(1)}, bf16[2,64,64]{1,2,0:T(8,128)(2,1)S(1)}, f32[2,64]{1,0:T(2,128)S(1)}, ...) while((s32[]{:T(128)}, f32[130,256]{1,0:T(8,128)}, ...), condition=%wide.region_12.11_spmd, body=%wide.region_3.10_spmd.sunk | while | flops 118146688 | bytes 2256769 | solution.py:145
  1420.1 72.9 %all_to_all.80 = bf16[16,8,192]{2,1,0:T(8,128)(2,1)S(1)} all-to-all(bf16[16,8,192]{2,1,0:T(8,128)(2,1)S(1)} %fusion.83), channel_id=1, replica_groups=mesh['head'=16,'seq'=32] {'head'}, dimensions={0} | all-to-all | bytes 98304 | tf_op jit(solution)/shard_map/all_to_all | solution.py:258
  (713 shorter events, 401.5 us)
Async XLA Ops:
  1.6 25.6 %all-to-all-start.1 = ((bf16[8,16,192]{2,0,1:T(8,128)(2,1)}), bf16[8,16,192]{2,0,1:T(8,128)(2,1)S(1)}, u32[]{:S(2)}, u32[]{:S(2)}) async-start(bf16[8,16,192]{2,0,1:T(8,128)(2,1)} %copy.40), calls=%async_computation.1 | async-start | bytes 131072 | tf_op jit(solution)/shard_map/all_to_all | solution.py:166
  27.2 18.3 %all-to-all-start.2 = ((bf16[8,16,192]{2,0,1:T(8,128)(2,1)}), bf16[8,16,192]{2,0,1:T(8,128)(2,1)S(1)}, u32[]{:S(2)}, u32[]{:S(2)}) async-start(bf16[8,16,192]{2,0,1:T(8,128)(2,1)} %copy.41), calls=%async_computation.2 | async-start | bytes 131072 | tf_op jit(solution)/shard_map/all_to_all | solution.py:167
  45.5 18.3 %all-to-all-start.3 = ((bf16[8,16,192]{2,0,1:T(8,128)(2,1)}), bf16[8,16,192]{2,0,1:T(8,128)(2,1)S(1)}, u32[]{:S(2)}, u32[]{:S(2)}) async-start(bf16[8,16,192]{2,0,1:T(8,128)(2,1)} %copy.42), calls=%async_computation.3 | async-start | bytes 131072 | tf_op jit(solution)/shard_map/all_to_all | solution.py:168
  63.8 1356.3 %all-to-all-start = ((bf16[8,16,192]{2,0,1:T(8,128)(2,1)}), bf16[8,16,192]{2,0,1:T(8,128)(2,1)S(1)}, u32[]{:S(2)}, u32[]{:S(2)}) async-start(bf16[8,16,192]{2,0,1:T(8,128)(2,1)} %copy.39), calls=%async_computation | async-start | bytes 131072 | tf_op jit(solution)/shard_map/all_to_all | solution.py:169
  98.0 7.1 collective-permute-start
  134.6 6.0 collective-permute-start
  170.6 6.0 collective-permute-start
  177.3 31.3 %collective-permute-start.1 = (f32[130,256]{1,0:T(8,128)}, f32[130,256]{1,0:T(8,128)S(1)}, u32[]{:S(2)}, u32[]{:S(2)}) collective-permute-start(f32[130,256]{1,0:T(8,128)} %get-tuple-element.963), channel_id=1, source_target_pairs={{1,0},{2,1},{3,2},{4,3},{5,4},{6,5},{7,6},{8,7},{9,8},{10,9},{11,1... | collective-permute-start | bytes 399368 | tf_op jit(solution)/shard_map/while/body/eval_jaxpr/ppermute | solution.py:20
  206.9 6.0 collective-permute-start
  216.5 31.0 %collective-permute-start = (f32[130,256]{1,0:T(8,128)}, f32[130,256]{1,0:T(8,128)S(1)}, u32[]{:S(2)}, u32[]{:S(2)}) collective-permute-start(f32[130,256]{1,0:T(8,128)} %get-tuple-element.962), channel_id=1, source_target_pairs={{0,1},{1,2},{2,3},{3,4},{4,5},{5,6},{6,7},{7,8},{8,9},{9,10},{10,1... | collective-permute-start | bytes 399368 | tf_op jit(solution)/shard_map/while/body/eval_jaxpr/ppermute | solution.py:20
  252.2 6.0 collective-permute-start
  258.9 32.8 %collective-permute-start.1 = (f32[130,256]{1,0:T(8,128)}, f32[130,256]{1,0:T(8,128)S(1)}, u32[]{:S(2)}, u32[]{:S(2)}) collective-permute-start(f32[130,256]{1,0:T(8,128)} %get-tuple-element.963), channel_id=1, source_target_pairs={{1,0},{2,1},{3,2},{4,3},{5,4},{6,5},{7,6},{8,7},{9,8},{10,9},{11,1... | collective-permute-start | bytes 399368 | tf_op jit(solution)/shard_map/while/body/eval_jaxpr/ppermute | solution.py:20
  290.1 6.0 collective-permute-start
  296.8 6.3 collective-permute-start.1
  301.5 31.0 %collective-permute-start = (f32[130,256]{1,0:T(8,128)}, f32[130,256]{1,0:T(8,128)S(1)}, u32[]{:S(2)}, u32[]{:S(2)}) collective-permute-start(f32[130,256]{1,0:T(8,128)} %get-tuple-element.962), channel_id=1, source_target_pairs={{0,1},{1,2},{2,3},{3,4},{4,5},{5,6},{6,7},{7,8},{8,9},{9,10},{10,1... | collective-permute-start | bytes 399368 | tf_op jit(solution)/shard_map/while/body/eval_jaxpr/ppermute | solution.py:20
  333.2 7.8 collective-permute-start.1
  339.3 6.3 collective-permute-start
  346.3 26.9 %collective-permute-start.1 = (f32[130,256]{1,0:T(8,128)}, f32[130,256]{1,0:T(8,128)S(1)}, u32[]{:S(2)}, u32[]{:S(2)}) collective-permute-start(f32[130,256]{1,0:T(8,128)} %get-tuple-element.963), channel_id=1, source_target_pairs={{1,0},{2,1},{3,2},{4,3},{5,4},{6,5},{7,6},{8,7},{9,8},{10,9},{11,1... | collective-permute-start | bytes 399368 | tf_op jit(solution)/shard_map/while/body/eval_jaxpr/ppermute | solution.py:20
  378.1 7.8 collective-permute-start.1
  384.3 27.5 %collective-permute-start = (f32[130,256]{1,0:T(8,128)}, f32[130,256]{1,0:T(8,128)S(1)}, u32[]{:S(2)}, u32[]{:S(2)}) collective-permute-start(f32[130,256]{1,0:T(8,128)} %get-tuple-element.962), channel_id=1, source_target_pairs={{0,1},{1,2},{2,3},{3,4},{4,5},{5,6},{6,7},{7,8},{8,9},{9,10},{10,1... | collective-permute-start | bytes 399368 | tf_op jit(solution)/shard_map/while/body/eval_jaxpr/ppermute | solution.py:20
  412.4 7.8 collective-permute-start.1
  418.6 6.0 collective-permute-start
  425.2 27.2 %collective-permute-start.1 = (f32[130,256]{1,0:T(8,128)}, f32[130,256]{1,0:T(8,128)S(1)}, u32[]{:S(2)}, u32[]{:S(2)}) collective-permute-start(f32[130,256]{1,0:T(8,128)} %get-tuple-element.963), channel_id=1, source_target_pairs={{1,0},{2,1},{3,2},{4,3},{5,4},{6,5},{7,6},{8,7},{9,8},{10,9},{11,1... | collective-permute-start | bytes 399368 | tf_op jit(solution)/shard_map/while/body/eval_jaxpr/ppermute | solution.py:20
  450.7 6.0 collective-permute-start
  457.4 8.8 collective-permute-start.1
  463.5 29.6 %collective-permute-start = (f32[130,256]{1,0:T(8,128)}, f32[130,256]{1,0:T(8,128)S(1)}, u32[]{:S(2)}, u32[]{:S(2)}) collective-permute-start(f32[130,256]{1,0:T(8,128)} %get-tuple-element.962), channel_id=1, source_target_pairs={{0,1},{1,2},{2,3},{3,4},{4,5},{5,6},{6,7},{7,8},{8,9},{9,10},{10,1... | collective-permute-start | bytes 399368 | tf_op jit(solution)/shard_map/while/body/eval_jaxpr/ppermute | solution.py:20
  493.8 7.8 collective-permute-start.1
  499.9 8.2 collective-permute-start
  508.7 25.0 %collective-permute-start.1 = (f32[130,256]{1,0:T(8,128)}, f32[130,256]{1,0:T(8,128)S(1)}, u32[]{:S(2)}, u32[]{:S(2)}) collective-permute-start(f32[130,256]{1,0:T(8,128)} %get-tuple-element.963), channel_id=1, source_target_pairs={{1,0},{2,1},{3,2},{4,3},{5,4},{6,5},{7,6},{8,7},{9,8},{10,9},{11,1... | collective-permute-start | bytes 399368 | tf_op jit(solution)/shard_map/while/body/eval_jaxpr/ppermute | solution.py:20
  532.1 6.0 collective-permute-start
  538.8 10.7 collective-permute-start.1
  547.8 24.5 %collective-permute-start = (f32[130,256]{1,0:T(8,128)}, f32[130,256]{1,0:T(8,128)S(1)}, u32[]{:S(2)}, u32[]{:S(2)}) collective-permute-start(f32[130,256]{1,0:T(8,128)} %get-tuple-element.962), channel_id=1, source_target_pairs={{0,1},{1,2},{2,3},{3,4},{4,5},{5,6},{6,7},{7,8},{8,9},{9,10},{10,1... | collective-permute-start | bytes 399368 | tf_op jit(solution)/shard_map/while/body/eval_jaxpr/ppermute | solution.py:20
  573.0 7.8 collective-permute-start.1
  579.2 7.7 collective-permute-start
  587.6 25.4 %collective-permute-start.1 = (f32[130,256]{1,0:T(8,128)}, f32[130,256]{1,0:T(8,128)S(1)}, u32[]{:S(2)}, u32[]{:S(2)}) collective-permute-start(f32[130,256]{1,0:T(8,128)} %get-tuple-element.963), channel_id=1, source_target_pairs={{1,0},{2,1},{3,2},{4,3},{5,4},{6,5},{7,6},{8,7},{9,8},{10,9},{11,1... | collective-permute-start | bytes 399368 | tf_op jit(solution)/shard_map/while/body/eval_jaxpr/ppermute | solution.py:20
  618.0 8.3 collective-permute-start.1
  624.7 29.0 %collective-permute-start = (f32[130,256]{1,0:T(8,128)}, f32[130,256]{1,0:T(8,128)S(1)}, u32[]{:S(2)}, u32[]{:S(2)}) collective-permute-start(f32[130,256]{1,0:T(8,128)} %get-tuple-element.962), channel_id=1, source_target_pairs={{0,1},{1,2},{2,3},{3,4},{4,5},{5,6},{6,7},{7,8},{8,9},{9,10},{10,1... | collective-permute-start | bytes 399368 | tf_op jit(solution)/shard_map/while/body/eval_jaxpr/ppermute | solution.py:20
  654.4 7.8 collective-permute-start.1
  660.6 8.0 collective-permute-start
  669.3 25.1 %collective-permute-start.1 = (f32[130,256]{1,0:T(8,128)}, f32[130,256]{1,0:T(8,128)S(1)}, u32[]{:S(2)}, u32[]{:S(2)}) collective-permute-start(f32[130,256]{1,0:T(8,128)} %get-tuple-element.963), channel_id=1, source_target_pairs={{1,0},{2,1},{3,2},{4,3},{5,4},{6,5},{7,6},{8,7},{9,8},{10,9},{11,1... | collective-permute-start | bytes 399368 | tf_op jit(solution)/shard_map/while/body/eval_jaxpr/ppermute | solution.py:20
  699.4 8.3 collective-permute-start.1
  706.0 27.0 %collective-permute-start = (f32[130,256]{1,0:T(8,128)}, f32[130,256]{1,0:T(8,128)S(1)}, u32[]{:S(2)}, u32[]{:S(2)}) collective-permute-start(f32[130,256]{1,0:T(8,128)} %get-tuple-element.962), channel_id=1, source_target_pairs={{0,1},{1,2},{2,3},{3,4},{4,5},{5,6},{6,7},{7,8},{8,9},{9,10},{10,1... | collective-permute-start | bytes 399368 | tf_op jit(solution)/shard_map/while/body/eval_jaxpr/ppermute | solution.py:20
  733.7 28.0 %collective-permute-start.1 = (f32[130,256]{1,0:T(8,128)}, f32[130,256]{1,0:T(8,128)S(1)}, u32[]{:S(2)}, u32[]{:S(2)}) collective-permute-start(f32[130,256]{1,0:T(8,128)} %get-tuple-element.963), channel_id=1, source_target_pairs={{1,0},{2,1},{3,2},{4,3},{5,4},{6,5},{7,6},{8,7},{9,8},{10,9},{11,1... | collective-permute-start | bytes 399368 | tf_op jit(solution)/shard_map/while/body/eval_jaxpr/ppermute | solution.py:20
  760.0 32.4 %collective-permute-start = (f32[130,256]{1,0:T(8,128)}, f32[130,256]{1,0:T(8,128)S(1)}, u32[]{:S(2)}, u32[]{:S(2)}) collective-permute-start(f32[130,256]{1,0:T(8,128)} %get-tuple-element.962), channel_id=1, source_target_pairs={{0,1},{1,2},{2,3},{3,4},{4,5},{5,6},{6,7},{7,8},{8,9},{9,10},{10,1... | collective-permute-start | bytes 399368 | tf_op jit(solution)/shard_map/while/body/eval_jaxpr/ppermute | solution.py:20
  793.0 62.2 %collective-permute-start.1 = (f32[130,256]{1,0:T(8,128)}, f32[130,256]{1,0:T(8,128)S(1)}, u32[]{:S(2)}, u32[]{:S(2)}) collective-permute-start(f32[130,256]{1,0:T(8,128)} %get-tuple-element.963), channel_id=1, source_target_pairs={{1,0},{2,1},{3,2},{4,3},{5,4},{6,5},{7,6},{8,7},{9,8},{10,9},{11,1... | collective-permute-start | bytes 399368 | tf_op jit(solution)/shard_map/while/body/eval_jaxpr/ppermute | solution.py:20
  853.6 32.4 %collective-permute-start = (f32[130,256]{1,0:T(8,128)}, f32[130,256]{1,0:T(8,128)S(1)}, u32[]{:S(2)}, u32[]{:S(2)}) collective-permute-start(f32[130,256]{1,0:T(8,128)} %get-tuple-element.962), channel_id=1, source_target_pairs={{0,1},{1,2},{2,3},{3,4},{4,5},{5,6},{6,7},{7,8},{8,9},{9,10},{10,1... | collective-permute-start | bytes 399368 | tf_op jit(solution)/shard_map/while/body/eval_jaxpr/ppermute | solution.py:20
  886.7 34.0 %collective-permute-start.1 = (f32[130,256]{1,0:T(8,128)}, f32[130,256]{1,0:T(8,128)S(1)}, u32[]{:S(2)}, u32[]{:S(2)}) collective-permute-start(f32[130,256]{1,0:T(8,128)} %get-tuple-element.963), channel_id=1, source_target_pairs={{1,0},{2,1},{3,2},{4,3},{5,4},{6,5},{7,6},{8,7},{9,8},{10,9},{11,1... | collective-permute-start | bytes 399368 | tf_op jit(solution)/shard_map/while/body/eval_jaxpr/ppermute | solution.py:20
  919.0 57.4 %collective-permute-start = (f32[130,256]{1,0:T(8,128)}, f32[130,256]{1,0:T(8,128)S(1)}, u32[]{:S(2)}, u32[]{:S(2)}) collective-permute-start(f32[130,256]{1,0:T(8,128)} %get-tuple-element.962), channel_id=1, source_target_pairs={{0,1},{1,2},{2,3},{3,4},{4,5},{5,6},{6,7},{7,8},{8,9},{9,10},{10,1... | collective-permute-start | bytes 399368 | tf_op jit(solution)/shard_map/while/body/eval_jaxpr/ppermute | solution.py:20
  977.1 35.4 %collective-permute-start.1 = (f32[130,256]{1,0:T(8,128)}, f32[130,256]{1,0:T(8,128)S(1)}, u32[]{:S(2)}, u32[]{:S(2)}) collective-permute-start(f32[130,256]{1,0:T(8,128)} %get-tuple-element.963), channel_id=1, source_target_pairs={{1,0},{2,1},{3,2},{4,3},{5,4},{6,5},{7,6},{8,7},{9,8},{10,9},{11,1... | collective-permute-start | bytes 399368 | tf_op jit(solution)/shard_map/while/body/eval_jaxpr/ppermute | solution.py:20
  1010.9 32.4 %collective-permute-start = (f32[130,256]{1,0:T(8,128)}, f32[130,256]{1,0:T(8,128)S(1)}, u32[]{:S(2)}, u32[]{:S(2)}) collective-permute-start(f32[130,256]{1,0:T(8,128)} %get-tuple-element.962), channel_id=1, source_target_pairs={{0,1},{1,2},{2,3},{3,4},{4,5},{5,6},{6,7},{7,8},{8,9},{9,10},{10,1... | collective-permute-start | bytes 399368 | tf_op jit(solution)/shard_map/while/body/eval_jaxpr/ppermute | solution.py:20
  1044.0 34.2 %collective-permute-start.1 = (f32[130,256]{1,0:T(8,128)}, f32[130,256]{1,0:T(8,128)S(1)}, u32[]{:S(2)}, u32[]{:S(2)}) collective-permute-start(f32[130,256]{1,0:T(8,128)} %get-tuple-element.963), channel_id=1, source_target_pairs={{1,0},{2,1},{3,2},{4,3},{5,4},{6,5},{7,6},{8,7},{9,8},{10,9},{11,1... | collective-permute-start | bytes 399368 | tf_op jit(solution)/shard_map/while/body/eval_jaxpr/ppermute | solution.py:20
  1076.5 32.5 %collective-permute-start = (f32[130,256]{1,0:T(8,128)}, f32[130,256]{1,0:T(8,128)S(1)}, u32[]{:S(2)}, u32[]{:S(2)}) collective-permute-start(f32[130,256]{1,0:T(8,128)} %get-tuple-element.962), channel_id=1, source_target_pairs={{0,1},{1,2},{2,3},{3,4},{4,5},{5,6},{6,7},{7,8},{8,9},{9,10},{10,1... | collective-permute-start | bytes 399368 | tf_op jit(solution)/shard_map/while/body/eval_jaxpr/ppermute | solution.py:20
  1109.6 34.2 %collective-permute-start.1 = (f32[130,256]{1,0:T(8,128)}, f32[130,256]{1,0:T(8,128)S(1)}, u32[]{:S(2)}, u32[]{:S(2)}) collective-permute-start(f32[130,256]{1,0:T(8,128)} %get-tuple-element.963), channel_id=1, source_target_pairs={{1,0},{2,1},{3,2},{4,3},{5,4},{6,5},{7,6},{8,7},{9,8},{10,9},{11,1... | collective-permute-start | bytes 399368 | tf_op jit(solution)/shard_map/while/body/eval_jaxpr/ppermute | solution.py:20
  1142.2 32.7 %collective-permute-start = (f32[130,256]{1,0:T(8,128)}, f32[130,256]{1,0:T(8,128)S(1)}, u32[]{:S(2)}, u32[]{:S(2)}) collective-permute-start(f32[130,256]{1,0:T(8,128)} %get-tuple-element.962), channel_id=1, source_target_pairs={{0,1},{1,2},{2,3},{3,4},{4,5},{5,6},{6,7},{7,8},{8,9},{9,10},{10,1... | collective-permute-start | bytes 399368 | tf_op jit(solution)/shard_map/while/body/eval_jaxpr/ppermute | solution.py:20
  1175.5 32.5 %collective-permute-start.1 = (f32[130,256]{1,0:T(8,128)}, f32[130,256]{1,0:T(8,128)S(1)}, u32[]{:S(2)}, u32[]{:S(2)}) collective-permute-start(f32[130,256]{1,0:T(8,128)} %get-tuple-element.963), channel_id=1, source_target_pairs={{1,0},{2,1},{3,2},{4,3},{5,4},{6,5},{7,6},{8,7},{9,8},{10,9},{11,1... | collective-permute-start | bytes 399368 | tf_op jit(solution)/shard_map/while/body/eval_jaxpr/ppermute | solution.py:20
  1206.4 32.4 %collective-permute-start = (f32[130,256]{1,0:T(8,128)}, f32[130,256]{1,0:T(8,128)S(1)}, u32[]{:S(2)}, u32[]{:S(2)}) collective-permute-start(f32[130,256]{1,0:T(8,128)} %get-tuple-element.962), channel_id=1, source_target_pairs={{0,1},{1,2},{2,3},{3,4},{4,5},{5,6},{6,7},{7,8},{8,9},{9,10},{10,1... | collective-permute-start | bytes 399368 | tf_op jit(solution)/shard_map/while/body/eval_jaxpr/ppermute | solution.py:20
  1239.4 34.2 %collective-permute-start.1 = (f32[130,256]{1,0:T(8,128)}, f32[130,256]{1,0:T(8,128)S(1)}, u32[]{:S(2)}, u32[]{:S(2)}) collective-permute-start(f32[130,256]{1,0:T(8,128)} %get-tuple-element.963), channel_id=1, source_target_pairs={{1,0},{2,1},{3,2},{4,3},{5,4},{6,5},{7,6},{8,7},{9,8},{10,9},{11,1... | collective-permute-start | bytes 399368 | tf_op jit(solution)/shard_map/while/body/eval_jaxpr/ppermute | solution.py:20
  1272.0 32.4 %collective-permute-start = (f32[130,256]{1,0:T(8,128)}, f32[130,256]{1,0:T(8,128)S(1)}, u32[]{:S(2)}, u32[]{:S(2)}) collective-permute-start(f32[130,256]{1,0:T(8,128)} %get-tuple-element.962), channel_id=1, source_target_pairs={{0,1},{1,2},{2,3},{3,4},{4,5},{5,6},{6,7},{7,8},{8,9},{9,10},{10,1... | collective-permute-start | bytes 399368 | tf_op jit(solution)/shard_map/while/body/eval_jaxpr/ppermute | solution.py:20
  1305.1 34.5 %collective-permute-start.1 = (f32[130,256]{1,0:T(8,128)}, f32[130,256]{1,0:T(8,128)S(1)}, u32[]{:S(2)}, u32[]{:S(2)}) collective-permute-start(f32[130,256]{1,0:T(8,128)} %get-tuple-element.963), channel_id=1, source_target_pairs={{1,0},{2,1},{3,2},{4,3},{5,4},{6,5},{7,6},{8,7},{9,8},{10,9},{11,1... | collective-permute-start | bytes 399368 | tf_op jit(solution)/shard_map/while/body/eval_jaxpr/ppermute | solution.py:20
  1338.3 6.0 collective-permute-start
  1344.9 32.9 %collective-permute-start.1 = (f32[130,256]{1,0:T(8,128)}, f32[130,256]{1,0:T(8,128)S(1)}, u32[]{:S(2)}, u32[]{:S(2)}) collective-permute-start(f32[130,256]{1,0:T(8,128)} %get-tuple-element.963), channel_id=1, source_target_pairs={{1,0},{2,1},{3,2},{4,3},{5,4},{6,5},{7,6},{8,7},{9,8},{10,9},{11,1... | collective-permute-start | bytes 399368 | tf_op jit(solution)/shard_map/while/body/eval_jaxpr/ppermute | solution.py:20
  1376.6 6.0 collective-permute-start
  1383.2 31.7 %collective-permute-start.1 = (f32[130,256]{1,0:T(8,128)}, f32[130,256]{1,0:T(8,128)S(1)}, u32[]{:S(2)}, u32[]{:S(2)}) collective-permute-start(f32[130,256]{1,0:T(8,128)} %get-tuple-element.963), channel_id=1, source_target_pairs={{1,0},{2,1},{3,2},{4,3},{5,4},{6,5},{7,6},{8,7},{9,8},{10,9},{11,1... | collective-permute-start | bytes 399368 | tf_op jit(solution)/shard_map/while/body/eval_jaxpr/ppermute | solution.py:20
  1413.7 6.0 collective-permute-start
  (18 other events, 162.7 us)
where the time goes:
time: 1500 us; the launch traced here: 1490 us
  starting transfers between devices  606 us (40%)
  waiting for transfers between devices  603 us (40%)
  matrix products  98.8 us (7%)
  local copies, waits for them, and re-layouts  76.8 us (5%)
  blocking collectives  72.9 us (5%)
  other arithmetic  33.5 us (2%)
    ppermute x68, starting transfers between devices, shifted(): return lax.ppermute(block, axis, route)  584 us
    ppermute x68, waiting for transfers between devices, shifted(): return lax.ppermute(block, axis, route)  562 us
    all_to_all x1, blocking collectives, local(): lax.all_to_all(gated, 'head', split_axis=0, concat_axis=1, tiled=True)  72.9 us
    another operation x64, local copies, waits for them, and re-layouts  40.7 us
  transfers between devices with their start and end apart: 72, of which 68 were waited for; matrix products, arithmetic and copies ran while one was open for 14% of the time, Pallas kernels for 0%

commit v1 on v0

v1 whole, which is shorter than its diff:
```python
import functools

import jax
import jax.numpy as jnp
from jax import lax
from jax.experimental import pallas as pl
from jax.experimental.pallas import tpu as pltpu
from jax.sharding import PartitionSpec as P

D_HEAD = 64
INNER = 256
MINI = 64
STEPS = 64
LANES = 128
GROUP = 16
CHAIN = 32
HEADS_LOCAL = 3
TILES = 24

EPS = 1e-06
ROOT = 0.7978845608028654
CUBE = 0.044715
MESH = pl.DeviceIdType.MESH
F32 = jnp.float32
BF16 = jnp.bfloat16

SEATS = ((4, 18, 24), (6, 12, 26))


def dot(left, right, dims):
    return lax.dot_general(
        left, right, (((dims[0],), (dims[1],)), ((), ())), preferred_element_type=F32
    )


def gelu(values):
    squared = values * values
    tanh_term = jnp.tanh(values * (ROOT + (ROOT * CUBE) * squared))
    return values * (0.5 + 0.5 * tanh_term)


def gelu_and_slope(values):
    squared = values * values
    tanh_term = jnp.tanh(values * (ROOT + (ROOT * CUBE) * squared))
    half = 0.5 + 0.5 * tanh_term
    slope = half + values * (half * (1.0 - tanh_term)) * (ROOT + (3.0 * ROOT * CUBE) * squared)
    return (values * half, slope)


def row_mean(values):
    return jnp.sum(values, axis=0, keepdims=True) * (1.0 / D_HEAD)


def lanes_left(rows):
    return lax.broadcasted_iota(jnp.int32, (rows, LANES), 1) < D_HEAD


def own_half(stacked):
    return jnp.where(lanes_left(D_HEAD), stacked[:D_HEAD], stacked[D_HEAD:])


def spread_halves(rows):
    left = lanes_left(D_HEAD)
    zero = jnp.zeros_like(rows)
    return jnp.concatenate([jnp.where(left, rows, zero), jnp.where(left, zero, rows)], axis=0)


def seat_of(core, place):
    return SEATS[0][place] + core * (SEATS[1][place] - SEATS[0][place])


def kernel(
    query_ref,
    key_ref,
    value_ref,
    gate_ref,
    rates_ref,
    first_ref,
    first_bias_ref,
    second_ref,
    second_bias_ref,
    gain_ref,
    shift_ref,
    out_ref,
    staged,
    gathered,
    packed,
    tokens,
    blocks_out,
    returned,
    relay_out,
    landed,
    kept_rows,
    bd_key,
    bd_query,
    rate_rows,
    target_rows,
    causal,
    halves,
    state_one,
    bias_one,
    state_two,
    state_two_turned,
    bias_two,
    gain_rows,
    shift_rows,
    pre_one_ref,
    dual_ref,
    act_ref,
    grad_two_ref,
    second_used,
    bias_used,
    send_a,
    recv_a,
    send_b,
    recv_b,
    send_c,
    recv_c,
    send_d,
    recv_d,
):
    head = lax.axis_index("head")
    seq = lax.axis_index("seq")
    core = lax.rem(head, 2)
    seats = [seat_of(core, place) for place in range(HEADS_LOCAL)]

    def is_seat(index):
        return jnp.logical_or(
            index == seats[0], jnp.logical_or(index == seats[1], index == seats[2])
        )

    seated = is_seat(seq)
    my_place = jnp.where(seq == seats[1], 1, 0) + jnp.where(seq == seats[2], 2, 0)

    barrier = pltpu.get_barrier_semaphore()

    @pl.loop(1, GROUP)
    def _(step):
        pl.semaphore_signal(
            barrier,
            inc=1,
            device_id=(lax.rem(head + step, GROUP), seq),
            device_id_type=MESH,
        )

    @pl.when(seated)
    def _():
        @pl.loop(1, CHAIN)
        def _(step):
            pl.semaphore_signal(
                barrier,
                inc=1,
                device_id=(head, lax.rem(seq + step, CHAIN)),
                device_id_type=MESH,
            )

    @pl.when(jnp.logical_not(seated))
    def _():
        for place in range(HEADS_LOCAL):
            pl.semaphore_signal(
                barrier, inc=1, device_id=(head, seats[place]), device_id_type=MESH
            )

    for tile in range(TILES):
        columns = slice(tile * LANES, (tile + 1) * LANES)
        staged[tile, 0] = query_ref[:, columns].astype(F32)
        staged[tile, 1] = key_ref[:, columns].astype(F32)
        staged[tile, 2] = value_ref[:, columns].astype(F32)

    @pl.when(seated)
    def _():
        pl.semaphore_wait(barrier, GROUP - 1 + CHAIN - 1)

    @pl.when(jnp.logical_not(seated))
    def _():
        pl.semaphore_wait(barrier, GROUP - 1 + HEADS_LOCAL)

    def first_tile(group):
        return (3 * group) // 2

    def exchange_copy(step):
        target = lax.rem(head + step, GROUP)
        return pltpu.make_async_remote_copy(
            src_ref=staged.at[pl.ds(first_tile(target), 2)],
            dst_ref=gathered.at[head],
            send_sem=send_a.at[target],
            recv_sem=recv_a.at[head],
            device_id=(target, seq),
            device_id_type=MESH,
        )

    @pl.loop(1, GROUP)
    def _(step):
        exchange_copy(step).start()

    gathered[head] = staged[pl.ds(first_tile(head), 2)]

    @pl.loop(1, GROUP)
    def _(step):
        source = lax.rem(head + GROUP - step, GROUP)
        pltpu.make_async_remote_copy(
            src_ref=staged.at[pl.ds(0, 2)],
            dst_ref=gathered.at[source],
            send_sem=send_a.at[source],
            recv_sem=recv_a.at[source],
            device_id=(source, seq),
            device_id_type=MESH,
        ).wait_recv()

    tall = CHAIN * 4
    lane = lax.broadcasted_iota(jnp.int32, (tall, LANES), 1)
    parity = core
    for place in range(HEADS_LOCAL):
        column = place + parity
        tile = column // 2
        half = lax.rem(column, 2)
        keys = gathered[:, tile, 1].reshape(tall, LANES)
        values = gathered[:, tile, 2].reshape(tall, LANES)
        queries = gathered[:, tile, 0].reshape(tall, LANES)
        at_left = half == 0
        keys_left = jnp.where(at_left, keys, pltpu.roll(keys, D_HEAD, 1))
        values_right = jnp.where(at_left, pltpu.roll(values, D_HEAD, 1), values)
        queries_left = jnp.where(at_left, queries, pltpu.roll(queries, D_HEAD, 1))
        rates = jnp.broadcast_to(rates_ref[:, place : place + 1], (tall, LANES))
        rates_high = rates.astype(BF16).astype(F32)
        rates_low = rates - rates_high
        rates_lanes = jnp.where(
            lane == D_HEAD, rates_high, jnp.where(lane == D_HEAD + 1, rates_low, 0.0)
        )
        packed[place, :, :LANES] = jnp.where(lane < D_HEAD, keys_left, values_right).astype(BF16)
        packed[place, :, LANES:] = jnp.where(lane < D_HEAD, queries_left, rates_lanes).astype(BF16)

    def relay_copy(place):
        return pltpu.make_async_remote_copy(
            src_ref=packed.at[place],
            dst_ref=tokens.at[seq],
            send_sem=send_b.at[place],
            recv_sem=recv_b.at[seq],
            device_id=(head, seats[place]),
            device_id_type=MESH,
        )

    for place in range(HEADS_LOCAL):

        @pl.when(seq != seats[place])
        def _():
            relay_copy(place).start()

    @pl.when(seated)
    def _():
        tokens[seq] = packed[my_place]

        row = lax.broadcasted_iota(jnp.int32, (LANES, LANES), 0)
        col = lax.broadcasted_iota(jnp.int32, (LANES, LANES), 1)
        ahead = jnp.logical_and(jnp.logical_and(row < 64, col < 64), row <= col)
        back = jnp.logical_and(jnp.logical_and(row >= 64, col >= 64), row >= col)
        causal[...] = jnp.where(jnp.logical_or(ahead, back), 1.0, 0.0)
        halves[...] = jnp.where((row < 64) == (col < 64), 1.0, 0.0)

        first = first_ref[my_place]
        both = jnp.concatenate([first, first], axis=0)
        state_one[...] = both.T
        second = second_ref[my_place]
        second = second - jnp.mean(second, axis=1, keepdims=True)
        doubled = jnp.concatenate([second, second], axis=1)
        state_two[...] = doubled
        state_two_turned[...] = doubled.T

        def spread_column(row_values, length):
            return jnp.broadcast_to(row_values, (LANES, length)).T

        bias_one[...] = spread_column(first_bias_ref[pl.ds(my_place, 1), :], INNER)
        second_bias = second_bias_ref[pl.ds(my_place, 1), :]
        second_bias = second_bias - jnp.mean(second_bias, axis=1, keepdims=True)
        bias_two[...] = spread_column(second_bias, D_HEAD)
        gain_rows[...] = spread_column(gain_ref[pl.ds(my_place, 1), :], D_HEAD)
        shift_rows[...] = spread_column(shift_ref[pl.ds(my_place, 1), :], D_HEAD)

        def await_block(block):
            @pl.when(block != seq)
            def _():
                pltpu.make_async_remote_copy(
                    src_ref=packed.at[0],
                    dst_ref=tokens.at[block],
                    send_sem=send_b.at[0],
                    recv_sem=recv_b.at[block],
                    device_id=(head, block),
                    device_id_type=MESH,
                ).wait_recv()

        def block_rows(step):
            return (step // 2, pl.multiple_of(lax.rem(step, 2) * MINI, MINI))

        sub = lax.broadcasted_iota(jnp.int32, (D_HEAD, LANES), 0)
        lan = lax.broadcasted_iota(jnp.int32, (D_HEAD, LANES), 1)
        minus_key = jnp.where(
            lan == sub + D_HEAD, 1.0, jnp.where(lan == sub, -1.0, 0.0)
        ).astype(BF16)
        pick_rate = jnp.where(
            jnp.logical_or(lan == D_HEAD, lan == D_HEAD + 1), 1.0, 0.0
        ).astype(BF16)
        eye_left = jnp.where(row == col, 1.0, 0.0).astype(BF16)

        def load_step(step):
            block_f, rows_f = block_rows(step)
            block_b, rows_b = block_rows(STEPS - 1 - step)
            kv_f = tokens[block_f, pl.ds(rows_f, MINI), :LANES]
            qr_f = tokens[block_f, pl.ds(rows_f, MINI), LANES:]
            kv_b = tokens[block_b, pl.ds(rows_b, MINI), :LANES]
            qr_b = tokens[block_b, pl.ds(rows_b, MINI), LANES:]
            left = lanes_left(MINI)

            def diagonal(ahead_rows, back_rows):
                turned = pltpu.roll(back_rows.astype(F32), D_HEAD, 1)
                return jnp.concatenate(
                    [jnp.where(left, ahead_rows.astype(F32), 0.0), jnp.where(left, 0.0, turned)],
                    axis=0,
                ).astype(BF16)

            keys_bd = diagonal(kv_f, kv_b)
            queries_bd = diagonal(qr_f, qr_b)
            target = dot(minus_key, jnp.concatenate([kv_f, kv_b], axis=0), (1, 1))
            rate = dot(pick_rate, jnp.concatenate([qr_f, qr_b], axis=0), (1, 1))
            return (keys_bd, queries_bd, target, rate)

        def store_step(loaded):
            bd_key[...] = loaded[0]
            bd_query[...] = loaded[1]
            target_rows[...] = gain_rows[...] * (shift_rows[...] - loaded[2])
            rate_rows[...] = loaded[3]

        def emit(step):
            dual_act = gelu(dual_ref[...]).astype(BF16)
            act = act_ref[...]
            attend = dot(act, dual_act, (0, 0))
            mask = causal[...]
            attend = (attend * mask + mask).astype(BF16)
            dual_two = (
                own_half(dot(second_used[...], dual_act, (1, 0)))
                + bias_used[...]
                - dot(grad_two_ref[...], attend, (1, 0))
            )
            centred = dual_two - row_mean(dual_two)
            spread = lax.rsqrt(row_mean(centred * centred) + EPS)
            fitted = gain_rows[...] * (centred * spread) + shift_rows[...]
            kept_rows[step] = fitted
            total = fitted + pltpu.roll(kept_rows[STEPS - 1 - step], D_HEAD, 1)
            total = jnp.concatenate([total, jnp.zeros_like(total)], axis=0).astype(BF16)
            turned = dot(eye_left, total, (1, 1)).astype(BF16)
            blocks_out[step] = turned[:MINI]
            blocks_out[STEPS - 1 - step] = turned[MINI:]

        def gradient(step):
            keys_bd = bd_key[...]
            queries_bd = bd_query[...]
            target = target_rows[...]
            rate = rate_rows[...]
            gain = gain_rows[...]
            second_now = state_two_turned[...]
            second_now_bf = second_now.astype(BF16)
            bias_two_now = bias_two[...]

            act, slope = gelu_and_slope(pre_one_ref[...])
            act = act.astype(BF16)
            pre_two = own_half(dot(second_now_bf, act, (1, 0))) + bias_two_now
            gain_sq = gain * gain
            mean_two = row_mean(pre_two)
            centred = pre_two - mean_two
            scaled = gain_sq * centred
            inverse = lax.rsqrt(row_mean(centred * centred) + EPS)
            mean_a = inverse * row_mean(scaled) + row_mean(target)
            mean_an = inverse * (
                inverse * row_mean(scaled * centred) + row_mean(target * centred)
            )
            grad_two = (
                scaled * inverse + target - mean_a - centred * (inverse * mean_an)
            ) * (inverse * rate)
            grad_two = grad_two.astype(BF16)
            grad_two_bd = spread_halves(grad_two)
            state_two_now = state_two[...]
            grad_one = dot(state_two_now.astype(BF16), grad_two_bd, (1, 0)) * slope
            grad_one = grad_one.astype(BF16)

            later = jnp.minimum(step + 1, STEPS - 1)
            loaded = load_step(later)
            ones_bd = halves[...]
            mask = causal[...]
            between = (dot(keys_bd, loaded[0], (1, 1)) + ones_bd).astype(BF16)
            within = (dot(keys_bd, queries_bd, (1, 1)) * mask + mask).astype(BF16)
            ones_bf = ones_bd.astype(BF16)
            fall = dot(grad_one, jnp.concatenate([between, keys_bd], axis=1), (1, 0))
            fall_out = dot(grad_one, jnp.concatenate([within, ones_bf], axis=1), (1, 0))

            state_one_now = state_one[...]
            high = state_one_now.astype(BF16)
            low = (state_one_now - high.astype(F32)).astype(BF16)
            reads = jnp.concatenate([loaded[0], queries_bd], axis=0)
            seen = dot(
                jnp.concatenate([high, low], axis=1),
                jnp.concatenate([reads, reads], axis=1),
                (1, 1),
            )
            bias_one_now = bias_one[...]
            pre_one_ref[...] = seen[:, :LANES] + bias_one_now - fall[:, :LANES]
            dual_ref[...] = seen[:, LANES:] + bias_one_now - fall_out[:, :LANES]
            state_one[...] = state_one_now - fall[:, LANES:]
            bias_one[...] = bias_one_now - fall_out[:, LANES:]
            state_two[...] = state_two_now - dot(act, grad_two_bd, (1, 1))
            state_two_turned[...] = second_now - dot(grad_two_bd, act, (1, 1))
            bias_two[...] = bias_two_now - dot(grad_two, ones_bf, (1, 0))
            act_ref[...] = act
            grad_two_ref[...] = grad_two
            second_used[...] = second_now_bf
            bias_used[...] = bias_two_now
            store_step(loaded)

        def return_copy(block):
            return pltpu.make_async_remote_copy(
                src_ref=blocks_out.at[pl.ds(2 * block, 2)],
                dst_ref=returned.at[my_place],
                send_sem=send_c.at[block],
                recv_sem=recv_c.at[my_place],
                device_id=(head, block),
                device_id_type=MESH,
            )

        def give_back(block):
            @pl.when(block != seq)
            def _():
                return_copy(block).start()

            @pl.when(block == seq)
            def _():
                returned[my_place] = blocks_out[pl.ds(2 * block, 2)]

        await_block(0)
        await_block(CHAIN - 1)
        begun = load_step(0)
        store_step(begun)
        high = state_one[...].astype(BF16)
        low = (state_one[...] - high.astype(F32)).astype(BF16)
        pre_one_ref[...] = (
            dot(high, begun[0], (1, 1)) + dot(low, begun[0], (1, 1)) + bias_one[...]
        )

        @pl.loop(0, STEPS)
        def _(step):
            later = step + 1

            @pl.when(jnp.logical_and(lax.rem(later, 2) == 0, later < STEPS // 2))
            def _():
                await_block(later // 2)
                await_block(CHAIN - 1 - later // 2)

            emit(jnp.maximum(step - 1, 0))
            gradient(step)

            done = step - 1

            @pl.when(jnp.logical_and(lax.rem(done, 2) == 1, done > STEPS // 2))
            def _():
                give_back(done // 2)
                give_back(CHAIN - 1 - done // 2)

        emit(STEPS - 1)
        give_back(CHAIN - 1)
        give_back(0)

        @pl.loop(1, CHAIN)
        def _(step):
            return_copy(lax.rem(seq + step, CHAIN)).wait_send()

    for place in range(HEADS_LOCAL):

        @pl.when(seq != seats[place])
        def _():
            pltpu.make_async_remote_copy(
                src_ref=blocks_out.at[pl.ds(0, 2)],
                dst_ref=returned.at[place],
                send_sem=send_c.at[0],
                recv_sem=recv_c.at[place],
                device_id=(head, seats[place]),
                device_id_type=MESH,
            ).wait_recv()

    shape = (GROUP, 8, LANES)
    zeros = jnp.zeros(shape, F32)
    parts = [returned[place].reshape(tall, LANES).astype(F32) for place in range(HEADS_LOCAL)]
    turned = [pltpu.roll(part, D_HEAD, 1) for part in parts]
    even = parity == 0
    relay_out[:, 0] = jnp.where(even, parts[0] + turned[1], turned[0]).reshape(shape)
    relay_out[:, 1] = jnp.where(even, parts[2], parts[1] + turned[2]).reshape(shape)

    def spread_copy(step):
        target = lax.rem(head + step, GROUP)
        return pltpu.make_async_remote_copy(
            src_ref=relay_out.at[target],
            dst_ref=landed.at[head],
            send_sem=send_d.at[target],
            recv_sem=recv_d.at[head],
            device_id=(target, seq),
            device_id_type=MESH,
        )

    @pl.loop(1, GROUP)
    def _(step):
        spread_copy(step).start()

    landed[head] = relay_out[head]

    @pl.loop(1, GROUP)
    def _(step):
        source = lax.rem(head + GROUP - step, GROUP)
        pltpu.make_async_remote_copy(
            src_ref=relay_out.at[source],
            dst_ref=landed.at[source],
            send_sem=send_d.at[source],
            recv_sem=recv_d.at[source],
            device_id=(source, seq),
            device_id_type=MESH,
        ).wait_recv()

    for pair in range(GROUP // 2):
        summed = (
            landed[2 * pair, 0],
            landed[2 * pair, 1] + landed[2 * pair + 1, 0],
            landed[2 * pair + 1, 1],
        )
        for tile in range(3):
            columns = slice((3 * pair + tile) * LANES, (3 * pair + tile + 1) * LANES)
            out_ref[:, columns] = (gate_ref[:, columns].astype(F32) * summed[tile]).astype(BF16)

    @pl.loop(1, GROUP)
    def _(step):
        exchange_copy(step).wait_send()
        spread_copy(step).wait_send()

    for place in range(HEADS_LOCAL):

        @pl.when(seq != seats[place])
        def _():
            relay_copy(place).wait_send()


def local(*arrays):
    vmem = pl.BlockSpec(memory_space=pltpu.VMEM)
    dma = pltpu.SemaphoreType.DMA
    return pl.pallas_call(
        kernel,
        out_shape=jax.ShapeDtypeStruct((8, TILES * LANES), BF16),
        in_specs=[vmem] * len(arrays),
        out_specs=vmem,
        scratch_shapes=[
            pltpu.VMEM((TILES, 3, 8, LANES), F32),
            pltpu.VMEM((GROUP, 2, 3, 8, LANES), F32),
            pltpu.VMEM((HEADS_LOCAL, 128, 2 * LANES), BF16),
            pltpu.VMEM((CHAIN, 128, 2 * LANES), BF16),
            pltpu.VMEM((STEPS, MINI, LANES), BF16),
            pltpu.VMEM((HEADS_LOCAL, 2, MINI, LANES), BF16),
            pltpu.VMEM((GROUP, 2, 8, LANES), F32),
            pltpu.VMEM((GROUP, 2, 8, LANES), F32),
            pltpu.VMEM((STEPS, D_HEAD, LANES), F32),
            pltpu.VMEM((LANES, LANES), BF16),
            pltpu.VMEM((LANES, LANES), BF16),
            pltpu.VMEM((D_HEAD, LANES), F32),
            pltpu.VMEM((D_HEAD, LANES), F32),
            pltpu.VMEM((LANES, LANES), F32),
            pltpu.VMEM((LANES, LANES), F32),
            pltpu.VMEM((INNER, LANES), F32),
            pltpu.VMEM((INNER, LANES), F32),
            pltpu.VMEM((INNER, LANES), F32),
            pltpu.VMEM((LANES, INNER), F32),
            pltpu.VMEM((D_HEAD, LANES), F32),
            pltpu.VMEM((D_HEAD, LANES), F32),
            pltpu.VMEM((D_HEAD, LANES), F32),
            pltpu.VMEM((INNER, LANES), F32),
            pltpu.VMEM((INNER, LANES), F32),
            pltpu.VMEM((INNER, LANES), BF16),
            pltpu.VMEM((D_HEAD, LANES), BF16),
            pltpu.VMEM((LANES, INNER), BF16),
            pltpu.VMEM((D_HEAD, LANES), F32),
            dma((GROUP,)),
            dma((GROUP,)),
            dma((HEADS_LOCAL,)),
            dma((CHAIN,)),
            dma((CHAIN,)),
            dma((HEADS_LOCAL,)),
            dma((GROUP,)),
            dma((GROUP,)),
        ],
        compiler_params=pltpu.CompilerParams(collective_id=0, has_side_effects=True),
    )(*arrays)


def solution(mesh):
    rows = P(("seq", "head"), None)
    in_specs = (
        rows,
        rows,
        rows,
        rows,
        P("seq", "head"),
        P("head", None, None),
        P("head", None),
        P("head", None, None),
        P("head", None),
        P("head", None),
        P("head", None),
    )
    return jax.shard_map(local, mesh=mesh, in_specs=in_specs, out_specs=rows, check_vma=False)
```

time: 1500 us -> 140 us (0.09)
  the two profiles are of different devices: /device:TPU:231 before, /device:TPU:1 now
where the time goes in v1:
time: 140 us
  Pallas kernels  135 us (96%)
  local copies, waits for them, and re-layouts  4.66 us (3%)
    pallas_call x1, Pallas kernels, local(): pl.pallas_call(kernel, out_shape=jax.ShapeDtypeStruct((8, TILES * LANES),...  135 us
    unnamed x3, local copies, waits for them, and re-layouts  4.66 us

profile of v1, /device:TPU:1, one launch (start us, length us, event | category | flops | bytes accessed | tf_op | source)
XLA Modules:
  0.0 139.7 jit_solution(9956809819532557212)
XLA Ops:
  0.0 1.4 %copy.12.rates_ref = f32[128,3]{1,0:T(8,128)} copy(f32[128,3]{0,1:T(4,128)} %param.15) | data formatting | bytes 3072 | tf_op args[4]
  1.4 1.8 %copy.13.second_ref = f32[3,256,64]{2,1,0:T(8,128)} copy(f32[3,256,64]{1,2,0:T(8,128)} %param.18) | data formatting | bytes 393216 | tf_op args[7]
  3.2 135.0 %shard_map.109 = bf16[8,3072]{1,0:T(8,128)(2,1)} custom-call(bf16[8,3072]{1,0:T(8,128)(2,1)} %query_ref.1, bf16[8,3072]{1,0:T(8,128)(2,1)} %key_ref.1, bf16[8,3072]{1,0:T(8,128)(2,1)} %value_ref.1, bf16[8,3072]{1,0:T(8,128)(2,1)} %gate_ref.1, f32[128,3]{1,0:T(8,128)} %copy.12.rates_ref, f32[3,64,256]{2,1,0:T(8,128)} %first_ref.1, f32[3,256]{1,0:T(4,128)} %first_bias_ref.1, ...), custom_call_target="tpu_custom_call" | custom-call | tf_op jit(solution)/shard_map/pallas_call | solution.py:548
  138.3 1.4 %copy.15 = bf16[8,3072]{1,0:T(8,128)(2,1)} copy(bf16[8,3072]{1,0:T(8,128)(2,1)} %shard_map.109) | data formatting | bytes 98304

commit v2 on v1

--- a/solution.py
+++ b/solution.py
@@ -48,6 +48,10 @@
 
 
 def row_mean(values):
+    rows = values.shape[0]
+    while rows > 8:
+        rows //= 2
+        values = values[:rows] + values[rows:]
     return jnp.sum(values, axis=0, keepdims=True) * (1.0 / D_HEAD)
 
 
@@ -92,7 +96,7 @@
     landed,
     kept_rows,
     bd_key,
-    bd_query,
+    turned_query,
     rate_rows,
     target_rows,
     causal,
@@ -100,7 +104,7 @@
     state_one,
     bias_one,
     state_two,
-    state_two_turned,
+    second_next,
     bias_two,
     gain_rows,
     shift_rows,
@@ -163,9 +167,9 @@
 
     for tile in range(TILES):
         columns = slice(tile * LANES, (tile + 1) * LANES)
-        staged[tile, 0] = query_ref[:, columns].astype(F32)
-        staged[tile, 1] = key_ref[:, columns].astype(F32)
-        staged[tile, 2] = value_ref[:, columns].astype(F32)
+        staged[tile, 0] = query_ref[:, columns]
+        staged[tile, 1] = key_ref[:, columns]
+        staged[tile, 2] = value_ref[:, columns]
 
     @pl.when(seated)
     def _():
@@ -214,14 +218,14 @@
         column = place + parity
         tile = column // 2
         half = lax.rem(column, 2)
-        keys = gathered[:, tile, 1].reshape(tall, LANES)
-        values = gathered[:, tile, 2].reshape(tall, LANES)
-        queries = gathered[:, tile, 0].reshape(tall, LANES)
+        keys = gathered[:, tile, 1].reshape(tall, LANES).astype(F32)
+        values = gathered[:, tile, 2].reshape(tall, LANES).astype(F32)
+        queries = gathered[:, tile, 0].reshape(tall, LANES).astype(F32)
         at_left = half == 0
         keys_left = jnp.where(at_left, keys, pltpu.roll(keys, D_HEAD, 1))
         values_right = jnp.where(at_left, pltpu.roll(values, D_HEAD, 1), values)
         queries_left = jnp.where(at_left, queries, pltpu.roll(queries, D_HEAD, 1))
-        rates = jnp.broadcast_to(rates_ref[:, place : place + 1], (tall, LANES))
+        rates = jnp.broadcast_to(rates_ref[place : place + 1], (LANES, tall)).T
         rates_high = rates.astype(BF16).astype(F32)
         rates_low = rates - rates_high
         rates_lanes = jnp.where(
@@ -261,10 +265,10 @@
         both = jnp.concatenate([first, first], axis=0)
         state_one[...] = both.T
         second = second_ref[my_place]
-        second = second - jnp.mean(second, axis=1, keepdims=True)
-        doubled = jnp.concatenate([second, second], axis=1)
-        state_two[...] = doubled
-        state_two_turned[...] = doubled.T
+        second = second - jnp.mean(second, axis=0, keepdims=True)
+        doubled = jnp.concatenate([second, second], axis=0)
+        state_two[...] = doubled.T
+        second_next[...] = doubled.astype(BF16)
 
         def spread_column(row_values, length):
             return jnp.broadcast_to(row_values, (LANES, length)).T
@@ -291,16 +295,6 @@
         def block_rows(step):
             return (step // 2, pl.multiple_of(lax.rem(step, 2) * MINI, MINI))
 
-        sub = lax.broadcasted_iota(jnp.int32, (D_HEAD, LANES), 0)
-        lan = lax.broadcasted_iota(jnp.int32, (D_HEAD, LANES), 1)
-        minus_key = jnp.where(
-            lan == sub + D_HEAD, 1.0, jnp.where(lan == sub, -1.0, 0.0)
-        ).astype(BF16)
-        pick_rate = jnp.where(
-            jnp.logical_or(lan == D_HEAD, lan == D_HEAD + 1), 1.0, 0.0
-        ).astype(BF16)
-        eye_left = jnp.where(row == col, 1.0, 0.0).astype(BF16)
-
         def load_step(step):
             block_f, rows_f = block_rows(step)
             block_b, rows_b = block_rows(STEPS - 1 - step)
@@ -309,108 +303,133 @@
             kv_b = tokens[block_b, pl.ds(rows_b, MINI), :LANES]
             qr_b = tokens[block_b, pl.ds(rows_b, MINI), LANES:]
             left = lanes_left(MINI)
-
-            def diagonal(ahead_rows, back_rows):
-                turned = pltpu.roll(back_rows.astype(F32), D_HEAD, 1)
-                return jnp.concatenate(
-                    [jnp.where(left, ahead_rows.astype(F32), 0.0), jnp.where(left, 0.0, turned)],
-                    axis=0,
-                ).astype(BF16)
-
-            keys_bd = diagonal(kv_f, kv_b)
-            queries_bd = diagonal(qr_f, qr_b)
-            target = dot(minus_key, jnp.concatenate([kv_f, kv_b], axis=0), (1, 1))
-            rate = dot(pick_rate, jnp.concatenate([qr_f, qr_b], axis=0), (1, 1))
-            return (keys_bd, queries_bd, target, rate)
+            turned_b = pltpu.roll(kv_b.astype(F32), D_HEAD, 1)
+            keys_bd = jnp.concatenate(
+                [jnp.where(left, kv_f.astype(F32), 0.0), jnp.where(left, 0.0, turned_b)], axis=0
+            ).astype(BF16)
+            kv_turned = jnp.concatenate([kv_f, kv_b], axis=0).T.astype(F32)
+            qr_turned = jnp.concatenate([qr_f, qr_b], axis=0).T.astype(F32)
+            target = kv_turned[D_HEAD:] - kv_turned[:D_HEAD]
+            rate = qr_turned[D_HEAD : D_HEAD + 1] + qr_turned[D_HEAD + 1 : D_HEAD + 2]
+            keys_turned = spread_halves(kv_turned[:D_HEAD]).astype(BF16)
+            queries_turned = spread_halves(qr_turned[:D_HEAD]).astype(BF16)
+            return (keys_bd, keys_turned, queries_turned, target, rate)
 
         def store_step(loaded):
             bd_key[...] = loaded[0]
-            bd_query[...] = loaded[1]
-            target_rows[...] = gain_rows[...] * (shift_rows[...] - loaded[2])
-            rate_rows[...] = loaded[3]
-
-        def emit(step):
-            dual_act = gelu(dual_ref[...]).astype(BF16)
-            act = act_ref[...]
-            attend = dot(act, dual_act, (0, 0))
-            mask = causal[...]
-            attend = (attend * mask + mask).astype(BF16)
-            dual_two = (
-                own_half(dot(second_used[...], dual_act, (1, 0)))
-                + bias_used[...]
-                - dot(grad_two_ref[...], attend, (1, 0))
-            )
-            centred = dual_two - row_mean(dual_two)
-            spread = lax.rsqrt(row_mean(centred * centred) + EPS)
-            fitted = gain_rows[...] * (centred * spread) + shift_rows[...]
+            turned_query[...] = loaded[2]
+            target_rows[...] = gain_rows[...] * (shift_rows[...] - loaded[3])
+            rate_rows[...] = jnp.broadcast_to(loaded[4], (8, LANES))
+
+        def finish(step, dual_two):
+            mean = row_mean(dual_two)
+            spread = lax.rsqrt(row_mean(dual_two * dual_two) - mean * mean + EPS)
+            fitted = gain_rows[...] * ((dual_two - mean) * spread) + shift_rows[...]
             kept_rows[step] = fitted
             total = fitted + pltpu.roll(kept_rows[STEPS - 1 - step], D_HEAD, 1)
             total = jnp.concatenate([total, jnp.zeros_like(total)], axis=0).astype(BF16)
-            turned = dot(eye_left, total, (1, 1)).astype(BF16)
+            turned = total.T
             blocks_out[step] = turned[:MINI]
             blocks_out[STEPS - 1 - step] = turned[MINI:]
 
-        def gradient(step):
-            keys_bd = bd_key[...]
-            queries_bd = bd_query[...]
+        def attend_dual(dual_act):
+            mask = causal[...]
+            read = dot(second_used[...], dual_act, (1, 0))
+            attend = dot(act_ref[...].T, dual_act, (1, 0))
+            return (own_half(read) + bias_used[...], (attend * mask + mask).astype(BF16))
+
+        def advance(step):
+            second_turned = second_next[...]
             target = target_rows[...]
-            rate = rate_rows[...]
             gain = gain_rows[...]
-            second_now = state_two_turned[...]
-            second_now_bf = second_now.astype(BF16)
+            gain_sq = gain * gain
+            rate = rate_rows[0:1]
             bias_two_now = bias_two[...]
 
             act, slope = gelu_and_slope(pre_one_ref[...])
             act = act.astype(BF16)
-            pre_two = own_half(dot(second_now_bf, act, (1, 0))) + bias_two_now
-            gain_sq = gain * gain
-            mean_two = row_mean(pre_two)
-            centred = pre_two - mean_two
-            scaled = gain_sq * centred
-            inverse = lax.rsqrt(row_mean(centred * centred) + EPS)
-            mean_a = inverse * row_mean(scaled) + row_mean(target)
+            pre_two = (
+                jnp.where(
+                    lanes_left(D_HEAD),
+                    dot(second_turned[:D_HEAD], act, (1, 0)),
+                    dot(second_turned[D_HEAD:], act, (1, 0)),
+                )
+                + bias_two_now
+            )
+
+            dual_act = gelu(dual_ref[...]).astype(BF16)
+            dual_read, attend = attend_dual(dual_act)
+
+            later = jnp.minimum(step + 1, STEPS - 1)
+            loaded = load_step(later)
+            keys_bd = bd_key[...]
+            queries_turned = turned_query[...]
+            ones_bd = halves[...]
+            ones_bf = ones_bd.astype(BF16)
+            mask = causal[...]
+            state_one_now = state_one[...]
+            high = state_one_now.astype(BF16)
+            low = (state_one_now - high.astype(F32)).astype(BF16)
+            reads = jnp.concatenate([loaded[1], queries_turned], axis=1)
+            reads = jnp.concatenate([reads, reads], axis=0)
+            within_both = dot(
+                jnp.concatenate([keys_bd, jnp.zeros_like(keys_bd)], axis=1), reads, (1, 0)
+            )
+            between = (within_both[:, :LANES] + ones_bd).astype(BF16)
+            within = (within_both[:, LANES:] * mask + mask).astype(BF16)
+            seen = dot(jnp.concatenate([high, low], axis=1), reads, (1, 0))
+
+            scaled = gain_sq * pre_two
+            mean = row_mean(pre_two)
+            sum_scaled = row_mean(scaled)
+            sum_square = row_mean(pre_two * pre_two)
+            sum_scaled_sq = row_mean(scaled * pre_two)
+            sum_target = row_mean(target * pre_two)
+            mean_gain = row_mean(gain_sq)
+            mean_target = row_mean(target)
+            inverse = lax.rsqrt(sum_square - mean * mean + EPS)
+            centred_scaled = sum_scaled - mean * mean_gain
+            mean_a = inverse * centred_scaled + mean_target
             mean_an = inverse * (
-                inverse * row_mean(scaled * centred) + row_mean(target * centred)
+                inverse * (sum_scaled_sq - mean * (sum_scaled + centred_scaled))
+                + (sum_target - mean * mean_target)
             )
+            weight = inverse * rate
             grad_two = (
-                scaled * inverse + target - mean_a - centred * (inverse * mean_an)
-            ) * (inverse * rate)
+                (pre_two - mean) * (inverse * gain_sq - inverse * mean_an) + (target - mean_a)
+            ) * weight
             grad_two = grad_two.astype(BF16)
             grad_two_bd = spread_halves(grad_two)
             state_two_now = state_two[...]
-            grad_one = dot(state_two_now.astype(BF16), grad_two_bd, (1, 0)) * slope
-            grad_one = grad_one.astype(BF16)
-
-            later = jnp.minimum(step + 1, STEPS - 1)
-            loaded = load_step(later)
-            ones_bd = halves[...]
-            mask = causal[...]
-            between = (dot(keys_bd, loaded[0], (1, 1)) + ones_bd).astype(BF16)
-            within = (dot(keys_bd, queries_bd, (1, 1)) * mask + mask).astype(BF16)
-            ones_bf = ones_bd.astype(BF16)
-            fall = dot(grad_one, jnp.concatenate([between, keys_bd], axis=1), (1, 0))
-            fall_out = dot(grad_one, jnp.concatenate([within, ones_bf], axis=1), (1, 0))
-
-            state_one_now = state_one[...]
-            high = state_one_now.astype(BF16)
-            low = (state_one_now - high.astype(F32)).astype(BF16)
-            reads = jnp.concatenate([loaded[0], queries_bd], axis=0)
-            seen = dot(
-                jnp.concatenate([high, low], axis=1),
-                jnp.concatenate([reads, reads], axis=1),
-                (1, 1),
-            )
-            bias_one_now = bias_one[...]
-            pre_one_ref[...] = seen[:, :LANES] + bias_one_now - fall[:, :LANES]
-            dual_ref[...] = seen[:, LANES:] + bias_one_now - fall_out[:, :LANES]
-            state_one[...] = state_one_now - fall[:, LANES:]
-            bias_one[...] = bias_one_now - fall_out[:, LANES:]
-            state_two[...] = state_two_now - dot(act, grad_two_bd, (1, 1))
-            state_two_turned[...] = second_now - dot(grad_two_bd, act, (1, 1))
+            state_two_bf = state_two_now.astype(BF16)
+            half = INNER // 2
+            grad_top = (dot(state_two_bf[:half], grad_two_bd, (1, 0)) * slope[:half]).astype(BF16)
+            grad_low = (dot(state_two_bf[half:], grad_two_bd, (1, 0)) * slope[half:]).astype(BF16)
+
+            dual_two = dual_read - dot(grad_two_ref[...], attend, (1, 0))
+            finish(jnp.maximum(step - 1, 0), dual_two)
+
+            state_two_new = state_two_now - dot(act, grad_two_bd.T, (1, 0))
             bias_two[...] = bias_two_now - dot(grad_two, ones_bf, (1, 0))
+            state_two[...] = state_two_new
+            second_next[...] = state_two_new.astype(BF16).T
+
+            moves = jnp.concatenate([between, keys_bd], axis=1)
+            sums = jnp.concatenate([within, ones_bf], axis=1)
+            for rows, part in ((slice(0, half), grad_top), (slice(half, INNER), grad_low)):
+                fall = dot(part, moves, (1, 0))
+                bias_one_now = bias_one[rows, :]
+                pre_one_ref[rows, :] = seen[rows, :LANES] + bias_one_now - fall[:, :LANES]
+                state_one[rows, :] = state_one_now[rows] - fall[:, LANES:]
+            for rows, part in ((slice(0, half), grad_top), (slice(half, INNER), grad_low)):
+                fall_out = dot(part, sums, (1, 0))
+                bias_one_now = bias_one[rows, :]
+                dual_ref[rows, :] = seen[rows, LANES:] + bias_one_now - fall_out[:, :LANES]
+                bias_one[rows, :] = bias_one_now - fall_out[:, LANES:]
+
             act_ref[...] = act
             grad_two_ref[...] = grad_two
-            second_used[...] = second_now_bf
+            second_used[...] = second_turned
             bias_used[...] = bias_two_now
             store_step(loaded)
 
@@ -440,7 +459,7 @@
         high = state_one[...].astype(BF16)
         low = (state_one[...] - high.astype(F32)).astype(BF16)
         pre_one_ref[...] = (
-            dot(high, begun[0], (1, 1)) + dot(low, begun[0], (1, 1)) + bias_one[...]
+            dot(high, begun[1], (1, 0)) + dot(low, begun[1], (1, 0)) + bias_one[...]
         )
 
         @pl.loop(0, STEPS)
@@ -452,8 +471,7 @@
                 await_block(later // 2)
                 await_block(CHAIN - 1 - later // 2)
 
-            emit(jnp.maximum(step - 1, 0))
-            gradient(step)
+            advance(step)
 
             done = step - 1
 
@@ -462,7 +480,8 @@
                 give_back(done // 2)
                 give_back(CHAIN - 1 - done // 2)
 
-        emit(STEPS - 1)
+        dual_read, attend = attend_dual(gelu(dual_ref[...]).astype(BF16))
+        finish(STEPS - 1, dual_read - dot(grad_two_ref[...], attend, (1, 0)))
         give_back(CHAIN - 1)
         give_back(0)
 
@@ -484,12 +503,11 @@
             ).wait_recv()
 
     shape = (GROUP, 8, LANES)
-    zeros = jnp.zeros(shape, F32)
     parts = [returned[place].reshape(tall, LANES).astype(F32) for place in range(HEADS_LOCAL)]
     turned = [pltpu.roll(part, D_HEAD, 1) for part in parts]
     even = parity == 0
-    relay_out[:, 0] = jnp.where(even, parts[0] + turned[1], turned[0]).reshape(shape)
-    relay_out[:, 1] = jnp.where(even, parts[2], parts[1] + turned[2]).reshape(shape)
+    relay_out[:, 0] = jnp.where(even, parts[0] + turned[1], turned[0]).astype(BF16).reshape(shape)
+    relay_out[:, 1] = jnp.where(even, parts[2], parts[1] + turned[2]).astype(BF16).reshape(shape)
 
     def spread_copy(step):
         target = lax.rem(head + step, GROUP)
@@ -521,11 +539,8 @@
         ).wait_recv()
 
     for pair in range(GROUP // 2):
-        summed = (
-            landed[2 * pair, 0],
-            landed[2 * pair, 1] + landed[2 * pair + 1, 0],
-            landed[2 * pair + 1, 1],
-        )
+        ends = [landed[2 * pair + side, tile].astype(F32) for side in (0, 1) for tile in (0, 1)]
+        summed = (ends[0], ends[1] + ends[2], ends[3])
         for tile in range(3):
             columns = slice((3 * pair + tile) * LANES, (3 * pair + tile + 1) * LANES)
             out_ref[:, columns] = (gate_ref[:, columns].astype(F32) * summed[tile]).astype(BF16)
@@ -543,6 +558,9 @@
 
 
 def local(*arrays):
+    arrays = list(arrays)
+    arrays[4] = arrays[4].T
+    arrays[7] = jnp.swapaxes(arrays[7], 1, 2)
     vmem = pl.BlockSpec(memory_space=pltpu.VMEM)
     dma = pltpu.SemaphoreType.DMA
     return pl.pallas_call(
@@ -551,25 +569,25 @@
         in_specs=[vmem] * len(arrays),
         out_specs=vmem,
         scratch_shapes=[
-            pltpu.VMEM((TILES, 3, 8, LANES), F32),
-            pltpu.VMEM((GROUP, 2, 3, 8, LANES), F32),
+            pltpu.VMEM((TILES, 3, 8, LANES), BF16),
+            pltpu.VMEM((GROUP, 2, 3, 8, LANES), BF16),
             pltpu.VMEM((HEADS_LOCAL, 128, 2 * LANES), BF16),
             pltpu.VMEM((CHAIN, 128, 2 * LANES), BF16),
             pltpu.VMEM((STEPS, MINI, LANES), BF16),
             pltpu.VMEM((HEADS_LOCAL, 2, MINI, LANES), BF16),
-            pltpu.VMEM((GROUP, 2, 8, LANES), F32),
-            pltpu.VMEM((GROUP, 2, 8, LANES), F32),
+            pltpu.VMEM((GROUP, 2, 8, LANES), BF16),
+            pltpu.VMEM((GROUP, 2, 8, LANES), BF16),
             pltpu.VMEM((STEPS, D_HEAD, LANES), F32),
             pltpu.VMEM((LANES, LANES), BF16),
             pltpu.VMEM((LANES, LANES), BF16),
-            pltpu.VMEM((D_HEAD, LANES), F32),
+            pltpu.VMEM((8, LANES), F32),
             pltpu.VMEM((D_HEAD, LANES), F32),
             pltpu.VMEM((LANES, LANES), F32),
             pltpu.VMEM((LANES, LANES), F32),
             pltpu.VMEM((INNER, LANES), F32),
             pltpu.VMEM((INNER, LANES), F32),
             pltpu.VMEM((INNER, LANES), F32),
-            pltpu.VMEM((LANES, INNER), F32),
+            pltpu.VMEM((LANES, INNER), BF16),
             pltpu.VMEM((D_HEAD, LANES), F32),
             pltpu.VMEM((D_HEAD, LANES), F32),
             pltpu.VMEM((D_HEAD, LANES), F32),

time: 140 us -> 104 us (0.74)
  Pallas kernels: 135 us -> 102 us
  local copies, waits for them, and re-layouts: 4.66 us -> 1.42 us
    pallas_call x1, Pallas kernels: 135 us -> 102 us  [local(): pl.pallas_call(kernel, out_shape=jax.ShapeDtypeStruct((8, TILES * LANES),...]
    unnamed x3 -> x1, local copies, waits for them, and re-layouts: 4.66 us -> 1.42 us
where the time goes in v2:
time: 104 us
  Pallas kernels  102 us (98%)
  local copies, waits for them, and re-layouts  1.42 us (1%)
    pallas_call x1, Pallas kernels, local(): pl.pallas_call(kernel, out_shape=jax.ShapeDtypeStruct((8, TILES * LANES),...  102 us

profile of v2, /device:TPU:1, one launch (start us, length us, event | category | flops | bytes accessed | tf_op | source)
XLA Modules:
  0.0 103.9 jit_solution(6723771495741773228)
XLA Ops:
  0.0 102.5 %shard_map.109 = bf16[8,3072]{1,0:T(8,128)(2,1)} custom-call(bf16[8,3072]{1,0:T(8,128)(2,1)} %query_ref.1, bf16[8,3072]{1,0:T(8,128)(2,1)} %key_ref.1, bf16[8,3072]{1,0:T(8,128)(2,1)} %value_ref.1, bf16[8,3072]{1,0:T(8,128)(2,1)} %gate_ref.1, f32[3,128]{1,0:T(4,128)} %bitcast.3, f32[3,64,256]{2,1,0:T(8,128)} %first_ref.1, f32[3,256]{1,0:T(4,128)} %first_bias_ref.1, ...), custom_call_target="tpu_custom_call" | custom-call | tf_op jit(solution)/shard_map/pallas_call | solution.py:566
  102.5 1.4 %copy.13 = bf16[8,3072]{1,0:T(8,128)(2,1)} copy(bf16[8,3072]{1,0:T(8,128)(2,1)} %shard_map.109) | data formatting | bytes 98304
